TPU v7x, 32 devices: a whole 2x2x4 slice. The times are simulated.
32 devices in a mesh: layer: 4 (over y, x), strip: 8 (over z, core).
Axes of the slice: x: 2, y: 2, z: 4, core: 2. Of those that a mesh axis runs over, the one named last changes fastest.
Arguments:
- launch: bfloat16 [2, 2, 1024, 1024], P(None, None, 'strip'), may hold values from -6 to 6
- screens: float32 [4, 1024, 1024], P('layer', 'strip'), may hold values from -3.140625 to 3.140625
- distance: float32 [4], P('layer'), may hold values from 1024 to 2048
- templates: bfloat16 [1024, 16], replicated, may hold values from -0.1875 to 0.1875
- send_table: int32 [8, 8, 4], P('strip', None, 'layer'), may hold values from 0 to 511, as said below
- send_counts: int32 [8, 8], P('strip'), may hold values from 0 to 4, as said below
Outputs:
- pupil: bfloat16 [2, 2, 1024, 1024], P(None, None, 'strip')
- correlation: float32 [8, 8, 4, 2, 16], P('strip', None, 'layer')
Inputs may be any that keep to these rules, and one draw needn't show every extreme that they name: For each source strip s the 8 x 4 entries send_table[s] are distinct subaperture numbers local to that strip (row by row over its 512 subapertures). `send_counts`: some owner receives 4 live slots from every source.
All inputs are finite; a program needn't handle non-finite values.
Results may differ from a plain program's by a relative error of at most 0.03.
Values may be sent and summed in bfloat16 or wider, within the bound.
A program may use at most 64 MiB of HBM per device.

v0:
```python
import functools
import math

import jax
import jax.numpy as jnp
import numpy as np
from jax import lax
from jax.experimental import pallas as pl
from jax.experimental.pallas import tpu as pltpu
from jax.sharding import PartitionSpec as P

SUB = 16
F32 = jnp.float32
BF16 = jnp.bfloat16
MESH = pl.DeviceIdType.MESH


def cosine_half_table(length):
    k = np.arange(length // 2, dtype=np.int64)
    n = np.arange(length, dtype=np.int64)
    p = (k[:, None] * n[None, :]) % length
    p = np.minimum(p, length - p)
    return np.cos(2.0 * np.pi * p / length).astype(np.float32).astype(BF16)


def spot_table(subsize):
    spotsize = 2 * subsize
    outer = np.arange(spotsize)
    inner = np.arange(subsize)
    angles = (inner[:, None] * outer[None, :] % spotsize) * (2.0 * np.pi / spotsize)
    wave = (np.cos(angles) - 1j * np.sin(angles)) / math.sqrt(subsize)
    kron = wave[:, None, :, None] * wave[None, :, None, :]
    kron = kron.reshape(subsize * subsize, spotsize * spotsize)
    upper = np.concatenate([kron.real, kron.imag], axis=1)
    lower = np.concatenate([-kron.imag, kron.real], axis=1)
    return np.concatenate([upper, lower], axis=0).astype(np.float32).astype(BF16)


def kernel_line(distance_value, length):
    half = length // 2
    counter = jnp.arange(half + 1, dtype=jnp.int32).astype(F32)
    phases = -distance_value * math.pi * counter * counter / float(length * length)
    h = jnp.stack([jnp.cos(phases), jnp.sin(phases)])
    weight = jnp.where(counter == 0.0, 1.0, 2.0) / length
    folded = (h * weight)[:, :half]
    high = folded.astype(BF16)
    low = (folded - high.astype(F32)).astype(BF16)
    table = jnp.asarray(cosine_half_table(length))
    parts = jnp.dot(jnp.concatenate([high, low]), table, preferred_element_type=F32)
    sign = (1 - 2 * (jnp.arange(length, dtype=jnp.int32) % 2)).astype(F32) / length
    line = parts[:2] + parts[2:] + h[:, half:] * sign
    return jnp.concatenate([line, jnp.zeros((6, length), F32)])


def sincos(x):
    y = 0.5 * x
    z = y * y
    s = -1.0 / 39916800.0
    for c in (1.0 / 362880.0, -1.0 / 5040.0, 1.0 / 120.0, -1.0 / 6.0, 1.0):
        s = s * z + c
    s = s * y
    c0 = 1.0 / 479001600.0
    for c in (-1.0 / 3628800.0, 1.0 / 40320.0, -1.0 / 720.0, 1.0 / 24.0, -0.5, 1.0):
        c0 = c0 * z + c
    return 2.0 * s * c0, 1.0 - 2.0 * s * s


def propagate_kernel(
    layers, strips, launch_ref, scr_ref, scrt_ref, g_ref, out_ref,
    gall, gmat, early_row, early_col, stage_row, stage_col, srow, scol, sendbuf, recvbuf, slab, swapped, mid,
    gsend, grecv, ssend, srecv, xsend, xrecv, osend, orecv,
):
    count = layers * strips
    length = launch_ref.shape[-1]
    lines = launch_ref.shape[-2]
    wide = 4 * lines
    sec = lax.axis_index("layer")
    strip = lax.axis_index("strip")
    me = strip * layers + sec

    barrier = pltpu.get_barrier_semaphore()

    def greet(k, _):
        peer = lax.rem(me + k, count)
        pl.semaphore_signal(
            barrier, inc=1, device_id=(lax.rem(peer, layers), peer // layers), device_id_type=MESH
        )
        return 0

    lax.fori_loop(1, count, greet, 0)
    pl.semaphore_wait(barrier, count - 1)

    def remote(src, dst, ssem, rsem, a, s):
        return pltpu.make_async_remote_copy(
            src_ref=src, dst_ref=dst, send_sem=ssem, recv_sem=rsem,
            device_id=(a, s), device_id_type=MESH,
        )

    for k in range(1, layers):
        a = lax.rem(sec + k, layers)
        remote(g_ref, gall.at[sec], gsend, grecv.at[sec], a, strip).start()
    def to_all(start_one):
        def one(k, _):
            peer = lax.rem(me + k, count)
            start_one(lax.rem(peer, layers), peer // layers)
            return 0

        lax.fori_loop(1, count, one, 0)

    rows_of = [(stage_row, early_row)] + [(scr_ref, srow.at[i]) for i in range(layers // 2 - 1)]
    cols_of = [(stage_col, early_col)] + [(scrt_ref, scol.at[i]) for i in range(layers // 2 - 1)]

    def share(lay):
        @pl.when(sec == lay)
        def _():
            if lay % 2 == 0:
                src, dst = rows_of[lay // 2]
                if lay < 2:
                    src[...] = scr_ref[...].astype(BF16)
                for k in range(1, layers):
                    a = lax.rem(sec + k, layers)
                    remote(src.at[a], dst, ssend, srecv.at[lay], a, strip).start()
                dst[...] = src[lay]
            else:
                src, dst = cols_of[lay // 2]
                if lay < 2:
                    src[...] = scrt_ref[...].astype(BF16)

                def one(a, s):
                    remote(
                        src.at[s * layers + a], dst.at[strip], ssend, srecv.at[lay], a, s
                    ).start()

                to_all(one)
                dst[strip] = src[me]

    for lay in range(layers):
        share(lay)
    gall[sec] = g_ref[...]

    def build(lay):
        @pl.when(sec != lay)
        def _():
            remote(g_ref, gall.at[lay], gsend, grecv.at[lay], sec, strip).wait_recv()

        band = 128
        for part in range(2):
            row = gall[lay, part:part + 1, :]
            base = pltpu.roll(
                jnp.broadcast_to(row, (band, length)), 0, axis=1, stride=1, stride_axis=0
            ).astype(BF16)
            for b in range(length // band):
                at = band * b
                if b:
                    gmat[lay, part, at:at + band, 0:at] = base[:, length - at:]
                gmat[lay, part, at:at + band, at:] = base[:, :length - at]

    def screen_of(lay):
        if lay % 2 == 0:
            src, dst = rows_of[lay // 2]

            @pl.when(sec != lay)
            def _():
                remote(src.at[0], dst, ssend, srecv.at[lay], sec, strip).wait_recv()
            return sincos(dst[...].astype(F32))

        dst = cols_of[lay // 2][1]

        @pl.when(sec != lay)
        def _():
            remote(dst, dst, ssend, srecv.at[lay], sec, strip).wait_recv()

        @pl.when(sec == lay)
        def _():
            most = dst.at[pl.ds(0, strips - 1)]
            remote(most, most, ssend, srecv.at[lay], sec, strip).wait_recv()

        return sincos(jnp.concatenate([dst[s].astype(F32) for s in range(strips)], axis=1))

    def put(fc, value):
        rounded = value.astype(BF16)
        slab[fc * lines:(fc + 1) * lines, :] = rounded
        other = fc ^ 1
        swapped[other * lines:(other + 1) * lines, :] = rounded if fc % 2 == 0 else -rounded

    def screened(lay, load):
        sine, cosine = screen_of(lay)
        for f in range(2):
            re = load(2 * f)
            im = load(2 * f + 1)
            put(2 * f, re * cosine - im * sine)
            put(2 * f + 1, re * sine + im * cosine)

    block = 256

    def across(lay, step):
        per = block // lines

        def body(i, _):
            b = lax.rem(me // per + 1 + i, length // block)
            at = pl.ds(pl.multiple_of(b * block, block), block)
            dims = (((1,), (1,)), ((), ()))
            total = lax.dot_general(
                gmat[lay, 0, at, :], slab[...], dims, preferred_element_type=F32
            ) + lax.dot_general(
                gmat[lay, 1, at, :], swapped[...], dims, preferred_element_type=F32
            )
            sendbuf[step, pl.ds(b * per, per)] = total.reshape(per, lines, wide).astype(BF16)

            def one(j, _):
                peer = b * per + lax.rem(me + j, per)

                @pl.when(peer != me)
                def _():
                    remote(
                        sendbuf.at[step, peer], recvbuf.at[step, me], xsend.at[step],
                        xrecv.at[step], lax.rem(peer, layers), peer // layers,
                    ).start()
                return 0

            lax.fori_loop(0, per, one, 0)
            return 0

        lax.fori_loop(0, length // block, body, 0)

        recvbuf[step, me] = sendbuf[step, me]

    def arrived(step):
        most = recvbuf.at[step, pl.ds(0, count - 1)]
        remote(most, most, xsend.at[step], xrecv.at[step], sec, strip).wait_recv()
        if wide == 128:
            lane = lax.broadcasted_iota(jnp.int32, (lines, wide), 1) // lines
            for g in range(count // 4):
                pieces = [recvbuf[step, 4 * g + q].astype(F32) for q in range(4)]
                for fc in range(4):
                    out = None
                    for q in range(4):
                        shift = ((q - fc) * lines) % wide
                        moved = pltpu.roll(pieces[q], shift, axis=1) if shift else pieces[q]
                        out = moved if out is None else jnp.where(lane == q, moved, out)
                    rounded = out.astype(BF16)
                    at = slice(g * wide, (g + 1) * wide)
                    slab[fc * lines:(fc + 1) * lines, at] = rounded
                    other = fc ^ 1
                    swapped[other * lines:(other + 1) * lines, at] = (
                        rounded if fc % 2 == 0 else -rounded
                    )
        else:
            for fc in range(4):
                put(fc, jnp.concatenate(
                    [
                        recvbuf[step, d].astype(F32)[:, fc * lines:(fc + 1) * lines]
                        for d in range(count)
                    ],
                    axis=1,
                ))

    def along(lay):
        def body(b, _):
            at = pl.ds(pl.multiple_of(b * block, block), block)
            mid[:, at] = jnp.dot(
                slab[...], gmat[lay, 0, :, at], preferred_element_type=F32
            ) + jnp.dot(swapped[...], gmat[lay, 1, :, at], preferred_element_type=F32)
            return 0

        lax.fori_loop(0, length // block, body, 0)

    build(0)
    screened(0, lambda fc: launch_ref[fc, sec].astype(F32))
    across(0, 0)
    for lay in range(1, layers):
        build(lay)
    for lay in range(1, layers):
        arrived(lay - 1)
        along(lay - 1)
        screened(lay, lambda fc: mid[fc * lines:(fc + 1) * lines, :])
        across(lay, lay)
    arrived(layers - 1)
    along(layers - 1)
    for fc in range(4):
        out_ref[sec, fc] = mid[fc * lines:(fc + 1) * lines, :].astype(BF16)
    for k in range(1, layers):
        a = lax.rem(sec + k, layers)
        remote(out_ref.at[sec], out_ref.at[sec], osend, orecv, a, strip).start()
    most = out_ref.at[pl.ds(0, layers - 1)]
    remote(most, most, osend, orecv, sec, strip).wait()
    for k in range(1, layers):
        remote(g_ref, gall.at[sec], gsend, grecv.at[sec], sec, strip).wait_send()
    for lay in range(layers):
        @pl.when(sec == lay)
        def _(lay=lay):
            if lay % 2 == 0:
                some = rows_of[lay // 2][0].at[pl.ds(0, layers - 1)]
            else:
                some = cols_of[lay // 2][0].at[pl.ds(0, count - 1)]
            remote(some, some, ssend, srecv.at[lay], sec, strip).wait_send()
    for step in range(layers):
        most = sendbuf.at[step, pl.ds(0, count - 1)]
        remote(most, most, xsend.at[step], xrecv.at[step], sec, strip).wait_send()


def propagate(launch, screens, line, layers, strips):
    rows, length = launch.shape[2:]
    lines = rows // layers
    count = layers * strips
    vmem = pl.BlockSpec(memory_space=pltpu.VMEM)
    dma = pltpu.SemaphoreType.DMA
    screen = screens[0]
    return pl.pallas_call(
        functools.partial(propagate_kernel, layers, strips),
        out_shape=jax.ShapeDtypeStruct((layers, 4, lines, length), BF16),
        in_specs=[vmem] * 4,
        out_specs=vmem,
        scratch_shapes=[
            pltpu.VMEM((layers, 8, length), F32),
            pltpu.VMEM((layers, 2, length, length), BF16),
            pltpu.VMEM((lines, length), BF16),
            pltpu.VMEM((strips, lines, rows), BF16),
            pltpu.VMEM((layers, lines, length), BF16),
            pltpu.VMEM((count, lines, rows), BF16),
            pltpu.VMEM((layers // 2 - 1, lines, length), F32),
            pltpu.VMEM((layers // 2 - 1, strips, lines, rows), F32),
            pltpu.VMEM((layers, count, lines, 4 * lines), BF16),
            pltpu.VMEM((layers, count, lines, 4 * lines), BF16),
            pltpu.VMEM((4 * lines, length), BF16),
            pltpu.VMEM((4 * lines, length), BF16),
            pltpu.VMEM((4 * lines, length), F32),
            dma, dma((layers,)), dma, dma((layers,)), dma((layers,)), dma((layers,)), dma, dma,
        ],
        compiler_params=pltpu.CompilerParams(
            collective_id=0, has_side_effects=True, vmem_limit_bytes=56 << 20
        ),
        name="propagate",
    )(
        launch.reshape(4, layers, lines, length),
        screen.reshape(layers, lines, length),
        screen.T.reshape(count, lines, rows),
        line,
    )


def gather_kernel(side, picks_ref, pupil_ref, out_ref):
    for o in range(out_ref.shape[0]):
        pick = picks_ref[o]
        top = pl.multiple_of(pick // side * SUB, SUB)
        left = pick % side * SUB
        tile = pl.multiple_of(left // 128 * 128, 128)
        shift = (128 - left % 128) % 128
        for part in range(4):
            rows = pupil_ref[part, pl.ds(top, SUB), pl.ds(tile, 128)].astype(F32)
            out_ref[o, part] = pltpu.roll(rows, shift, axis=1)[:, :SUB].astype(BF16)


def gather_blocks(pupil, picks):
    vmem = pl.BlockSpec(memory_space=pltpu.VMEM)
    return pl.pallas_call(
        functools.partial(gather_kernel, pupil.shape[-1] // SUB),
        out_shape=jax.ShapeDtypeStruct((picks.shape[0], 4, SUB, SUB), BF16),
        in_specs=[pl.BlockSpec(memory_space=pltpu.SMEM), vmem],
        out_specs=vmem,
        name="gather",
    )(picks, pupil)


def swap_kernel(strips, in_ref, out_ref, send, recv):
    sec = lax.axis_index("layer")
    strip = lax.axis_index("strip")
    barrier = pltpu.get_barrier_semaphore()
    for k in range(1, strips):
        pl.semaphore_signal(
            barrier, inc=1, device_id=(sec, lax.rem(strip + k, strips)), device_id_type=MESH
        )
    pl.semaphore_wait(barrier, strips - 1)
    for k in range(1, strips):
        peer = lax.rem(strip + k, strips)
        pltpu.make_async_remote_copy(
            src_ref=in_ref.at[peer], dst_ref=out_ref.at[strip], send_sem=send, recv_sem=recv,
            device_id=(sec, peer), device_id_type=MESH,
        ).start()
    out_ref[strip] = in_ref[strip]
    most = out_ref.at[pl.ds(0, strips - 1)]
    pltpu.make_async_remote_copy(
        src_ref=most, dst_ref=most, send_sem=send, recv_sem=recv,
        device_id=(sec, strip), device_id_type=MESH,
    ).wait()


def swap_strips(result, strips):
    fields, channels = result.shape[1:]
    vmem = pl.BlockSpec(memory_space=pltpu.VMEM)
    dma = pltpu.SemaphoreType.DMA
    out = pl.pallas_call(
        functools.partial(swap_kernel, strips),
        out_shape=jax.ShapeDtypeStruct((strips, 8, 128), F32),
        in_specs=[vmem],
        out_specs=vmem,
        scratch_shapes=[dma, dma],
        compiler_params=pltpu.CompilerParams(collective_id=1, has_side_effects=True),
        name="swap",
    )(jnp.pad(result, ((0, 0), (0, 8 - fields), (0, 128 - channels))))
    return out[:, :fields, :channels]


def per_device(launch, screens, distance, templates, send_table, send_counts):
    layers = lax.axis_size("layer")
    strips = lax.axis_size("strip")
    sec = lax.axis_index("layer")
    fields = launch.shape[0]
    rows, length = launch.shape[2:]
    line = kernel_line(distance[0], length)
    done = propagate(launch, screens, line, layers, strips)
    pupil = done.transpose(1, 0, 2, 3).reshape(fields, 2, rows, length)
    side = length // SUB
    blocks = gather_blocks(pupil.reshape(2 * fields, rows, length), send_table.reshape(strips))
    flat = blocks.reshape(strips * fields, 2 * SUB * SUB)
    table = jnp.asarray(spot_table(SUB))
    pixels = templates.shape[0]
    spot = jnp.dot(flat, table, preferred_element_type=F32)
    intensity = (spot[:, :pixels] ** 2 + spot[:, pixels:] ** 2).astype(BF16)
    result = jnp.dot(intensity, templates, preferred_element_type=F32)
    result = result.reshape(strips, fields, templates.shape[1])
    live = sec < send_counts[0]
    result = jnp.where(live[:, None, None], result, 0.0)
    received = swap_strips(result, strips)
    return (pupil, received[None, :, None])


def solution(mesh):
    placed = (
        P(None, None, "strip", None),
        P("layer", "strip", None),
        P("layer"),
        P(),
        P("strip", None, "layer"),
        P("strip", None),
    )
    return jax.shard_map(
        per_device,
        mesh=mesh,
        in_specs=placed,
        out_specs=(P(None, None, "strip", None), P("strip", None, "layer", None, None)),
        check_vma=False,
    )
```

profile of v0, /device:TPU:0, one launch (start us, length us, event | category | flops | bytes accessed | tf_op | source)
XLA Modules:
  0.0 92.9 jit_solution(404228109470664228)
XLA Ops:
  0.6 0.0 copy-start
  1.3 0.1 fusion.16
  1.4 1.5 %fusion.14 = f32[4,1024]{1,0:T(4,128)S(1)} fusion(bf16[512,1024]{1,0:T(8,128)(2,1)} %constant.48.clone, bf16[2,512]{1,0:T(2,128)(2,1)S(1)} %get-tuple-element.10, bf16[2,512]{1,0:T(2,128)(2,1)S(1)} %get-tuple-element.11), kind=kOutput, calls=%fused_computation.26 | convolution fusion | flops 4202496 | bytes 1069056 | tf_op jit(solution)/shard_map/dot_general | solution.py:49
  2.9 0.1 fusion.18
  3.0 0.1 fusion.4
  3.1 0.6 concatenate.7.g_ref
  3.8 2.0 %copy.21 = f32[1024,128]{1,0:T(8,128)} copy(f32[1024,128]{0,1:T(8,128)} %bitcast.27) | data formatting | bytes 1048576 | tf_op jit(solution)/shard_map/transpose | solution.py:337
  5.8 72.1 %propagate.1 = bf16[4,4,32,1024]{3,2,1,0:T(8,128)(2,1)} custom-call(bf16[4,4,32,1024]{3,2,1,0:T(8,128)(2,1)} %bitcast.30, f32[4,32,1024]{2,1,0:T(8,128)} %bitcast.28, f32[32,32,128]{2,1,0:T(8,128)} %bitcast.29, f32[8,1024]{1,0:T(8,128)} %concatenate.7.g_ref), custom_call_target="tpu_custom_call" | custom-call | tf_op jit(solution)/shard_map/propagate/pallas_call | solution.py:309
  77.9 0.0 copy-start.1
  77.9 2.4 %copy.22 = bf16[4,4,32,1024]{3,2,1,0:T(8,128)(2,1)} copy(bf16[4,4,32,1024]{3,2,0,1:T(8,128)(2,1)} %bitcast.24) | data formatting | bytes 2097152 | tf_op jit(solution)/shard_map/transpose | solution.py:412
  80.3 0.0 copy-start.2
  80.3 2.1 %gather.1 = bf16[8,4,16,16]{3,2,1,0:T(8,128)(2,1)} custom-call(s32[8]{0:T(128)} %bitcast.32, bf16[4,128,1024]{2,1,0:T(8,128)(2,1)} %bitcast.25), custom_call_target="tpu_custom_call" | custom-call | tf_op jit(solution)/shard_map/gather/pallas_call | solution.py:356
  82.4 1.1 %reshape.77 = bf16[16,512]{1,0:T(8,128)(2,1)S(1)} reshape(bf16[8,4,16,16]{3,2,1,0:T(8,128)(2,1)} %gather.1) | data formatting | bytes 32768 | tf_op jit(solution)/shard_map/reshape | solution.py:415
  83.5 0.0 copy-done.1
  83.5 0.4 fusion.20
  83.9 0.0 copy-done
  83.9 0.1 fusion.2
  84.0 0.0 copy-done.2
  84.0 0.1 broadcast_select_fusion
  84.1 0.6 pad.5.in_ref
  84.7 6.8 %swap.1 = f32[8,8,128]{2,1,0:T(8,128)} custom-call(f32[8,8,128]{2,1,0:T(8,128)} %pad.5.in_ref), custom_call_target="tpu_custom_call" | custom-call | tf_op jit(solution)/shard_map/swap/pallas_call | solution.py:392
  91.5 1.4 %slice_bitcast_fusion = f32[1,8,1,2,16]{4,3,2,1,0:T(2,128)} fusion(f32[8,8,128]{2,1,0:T(8,128)} %swap.1), kind=kLoop, calls=%fused_computation.7 | loop fusion | bytes 2048
  (5 shorter events, 0.0 us)
Async XLA Ops:
  0.6 83.3 %copy-start = (bf16[1024,16]{0,1:T(8,128)(2,1)S(1)}, bf16[1024,16]{0,1:T(8,128)(2,1)}, u32[]{:S(2)}) copy-start(bf16[1024,16]{0,1:T(8,128)(2,1)} %param.11) | copy-start | bytes 98308
  77.9 5.6 %copy-start.1 = (bf16[512,2048]{1,0:T(8,128)(2,1)S(1)}, bf16[512,2048]{1,0:T(8,128)(2,1)}, u32[]{:S(2)}) copy-start(bf16[512,2048]{1,0:T(8,128)(2,1)} %constant.49.clone) | copy-start | bytes 6291460
  80.3 3.7 %copy-start.2 = (s32[1,8]{1,0:T(1,128)S(1)}, s32[1,8]{1,0:T(1,128)}, u32[]{:S(2)}) copy-start(s32[1,8]{1,0:T(1,128)} %param.13) | copy-start | bytes 100
where the time goes:
time: 93.4 us; the launch traced here: 92.9 us
  Pallas kernels  80.9 us (87%)
  local copies, waits for them, and re-layouts  8.2 us (9%)
  matrix products  1.99 us (2%)
  between operations  1.36 us (1%)
    pallas_call x1, Pallas kernels, propagate(): pl.pallas_call(functools.partial(propagate_kernel, layers, strips), out_s...  72.1 us
    pallas_call x1, Pallas kernels, swap_strips(): pl.pallas_call(functools.partial(swap_kernel, strips), out_shape=jax.Shap...  6.79 us
    transpose x1, local copies, waits for them, and re-layouts, per_device(): pupil = done.transpose(1, 0, 2, 3).reshape(fields, 2, rows, length)  2.44 us
    pallas_call x1, Pallas kernels, gather_blocks(): pl.pallas_call(functools.partial(gather_kernel, pupil.shape[-1] // SUB),...  2.09 us
    transpose x1, local copies, waits for them, and re-layouts, propagate(): screen.T.reshape(count, lines, rows)  2.03 us

commit v1 on v0

--- a/solution.py
+++ b/solution.py
@@ -401,6 +401,604 @@
     return out[:, :fields, :channels]
 
 
+QUARTER = 256
+TILE = 128
+PIECE = 16
+
+
+def spot_rows(subsize):
+    table = np.asarray(spot_table(subsize))
+    split = table.reshape(2, subsize, subsize // 4, 2, 2, table.shape[1])
+    return split.transpose(2, 3, 0, 4, 1, 5).reshape(table.shape)
+
+
+def spread(x):
+    (r0, i0), (r1, i1), (r2, i2), (r3, i3) = x
+    er, ei, fr, fi = r0 + r2, i0 + i2, r1 + r3, i1 + i3
+    gr, gi, dr, di = r0 - r2, i0 - i2, r1 - r3, i1 - i3
+    return [(er + fr, ei + fi), (gr - di, gi + dr), (er - fr, ei - fi), (gr + di, gi - dr)]
+
+
+def collect(y):
+    (r0, i0), (r1, i1), (r2, i2), (r3, i3) = y
+    er, ei, fr, fi = r0 + r2, i0 + i2, r1 + r3, i1 + i3
+    gr, gi, dr, di = r0 - r2, i0 - i2, r1 - r3, i1 - i3
+    return [(er + fr, ei + fi), (gr + di, gi - dr), (er - fr, ei - fi), (gr - di, gi + dr)]
+
+
+def fused_kernel(
+    info_ref, templates_ref, launch_ref, screen_ref, cosine_ref, spot_ref, out_ref, corr_ref,
+    field, screen, cosine, spot, infos, lines_ref, gmat, stage, staget, screen0, columns, screen2,
+    sincos_ref, slab, swapped, ybuf, send1, recv1, send2, recv2, send3, recv3, send4, recv4,
+    mine, select, flat, results, answers,
+    lsem, isend, irecv, ssend, srecv, xsend, xrecv, osend, orecv, csend, crecv,
+):
+    layers, strips, count = 4, 8, 32
+    group = count // 2
+    sec = lax.axis_index("layer")
+    strip = lax.axis_index("strip")
+    me = strip * layers + sec
+    half = me // group
+    place = lax.rem(me, group)
+
+    screen1, screen3 = columns.at[pl.ds(0, strips)], columns.at[pl.ds(strips, strips)]
+
+    copies = [
+        pltpu.make_async_copy(screen_ref, screen, lsem.at[0]),
+        pltpu.make_async_copy(launch_ref.at[:, sec], field, lsem.at[1]),
+        pltpu.make_async_copy(cosine_ref, cosine, lsem.at[2]),
+        pltpu.make_async_copy(spot_ref, spot, lsem.at[3]),
+    ]
+    for copy in copies:
+        copy.start()
+
+    barrier = pltpu.get_barrier_semaphore()
+
+    def greet(k, _):
+        peer = lax.rem(me + k, count)
+        pl.semaphore_signal(
+            barrier, inc=1, device_id=(lax.rem(peer, layers), peer // layers), device_id_type=MESH
+        )
+        return 0
+
+    lax.fori_loop(1, count, greet, 0)
+
+    def remote(src, dst, ssem, rsem, dev):
+        return pltpu.make_async_remote_copy(
+            src_ref=src, dst_ref=dst, send_sem=ssem, recv_sem=rsem,
+            device_id=(lax.rem(dev, layers), dev // layers), device_id_type=MESH,
+        )
+
+    results[...] = jnp.zeros_like(results)
+    infos[sec] = info_ref[...]
+    copies[0].wait()
+
+    @pl.when(lax.rem(sec, 2) == 0)
+    def _():
+        stage[...] = screen[...].astype(BF16)
+
+    @pl.when(lax.rem(sec, 2) == 1)
+    def _():
+        staget[...] = screen[...].T.astype(BF16)
+
+    pl.semaphore_wait(barrier, count - 1)
+
+    for k in range(1, layers):
+        peer = strip * layers + lax.rem(sec + k, layers)
+        remote(info_ref, infos.at[sec], isend, irecv, peer).start()
+
+    @pl.when(sec == 0)
+    def _():
+        for k in range(1, layers):
+            remote(
+                stage.at[pl.ds(32 * k, 32)], screen0, ssend, srecv.at[0], strip * layers + k
+            ).start()
+        screen0[...] = stage[0:32, :]
+
+    def share_columns(dst, sem):
+        def one(k, _):
+            peer = lax.rem(me + k, count)
+            remote(
+                staget.at[pl.ds(pl.multiple_of(64 * lax.rem(peer, group), 64), 64)],
+                dst.at[strip], ssend, sem, peer,
+            ).start()
+            return 0
+
+        lax.fori_loop(1, count, one, 0)
+        dst[strip] = staget[pl.ds(pl.multiple_of(64 * place, 64), 64), :]
+
+    @pl.when(sec == 1)
+    def _():
+        share_columns(screen1, srecv.at[1])
+
+    @pl.when(sec == 2)
+    def _():
+        for k in range(4):
+            peer = group * (k // 2) + 2 * strip + k % 2
+            src = stage.at[pl.ds(64 * (k % 2), 64)]
+
+            @pl.when(peer != me)
+            def _(peer=peer, src=src):
+                remote(src, screen2, ssend, srecv.at[2], peer).start()
+
+            @pl.when(peer == me)
+            def _(src=src):
+                screen2[...] = src[...]
+
+    @pl.when(sec == 3)
+    def _():
+        share_columns(screen3, srecv.at[3])
+
+    most = infos.at[pl.ds(0, layers - 1)]
+    remote(most, most, isend, irecv, me).wait_recv()
+    copies[2].wait()
+
+    row8 = lax.broadcasted_iota(jnp.int32, (8, TILE), 0)
+    dist = infos[3, 8:16, :]
+    for lay in range(3):
+        dist = jnp.where(row8 // 2 == lay, infos[lay, 8:16, :], dist)
+    wide = jnp.concatenate([dist] * 4, axis=1)
+    turn = 0.5 / float(1024 * 1024)
+
+    def wave(d, squares):
+        t = d * (squares * turn)
+        t = t - jnp.round(t)
+        sine, cosine_ = sincos(t * (-2.0 * math.pi))
+        row = lax.broadcasted_iota(jnp.int32, d.shape, 0)
+        return jnp.where(row % 2 == 0, cosine_, sine)
+
+    k = lax.broadcasted_iota(jnp.int32, (8, 512), 1).astype(F32)
+    weight = jnp.where(k == 0.0, 0.25, 0.5) / 1024.0
+    folded = wave(wide, k * k) * weight
+    high = folded.astype(BF16)
+    low = (folded - high.astype(F32)).astype(BF16)
+    parts = jnp.dot(
+        jnp.concatenate([high.astype(F32), low.astype(F32)], axis=0).astype(BF16),
+        cosine[...], preferred_element_type=F32,
+    )
+    last = wave(dist, jnp.full((8, TILE), 512.0 * 512.0, F32)) * (0.25 / 1024.0)
+    lane8 = lax.broadcasted_iota(jnp.int32, (8, TILE), 1)
+    last = jnp.where(lane8 % 2 == 0, last, -last)
+    lines_ref[...] = parts[:8] + parts[8:] + jnp.concatenate([last] * 8, axis=1)
+
+    def build(lay):
+        quarters = []
+        for q in range(4):
+            at = slice(QUARTER * q, QUARTER * (q + 1))
+            quarters.append((
+                lines_ref[2 * lay:2 * lay + 1, at], lines_ref[2 * lay + 1:2 * lay + 2, at]
+            ))
+        for b, (re, im) in enumerate(spread(quarters)):
+            turned = [(re, im), (-im, re), (-re, -im), (im, -re)][b]
+            for part, (first, second) in enumerate([(turned[0], re), (turned[1], im)]):
+                row = jnp.concatenate([first, second], axis=1)
+                base = pltpu.roll(
+                    jnp.broadcast_to(row, (TILE, 2 * QUARTER)), 0, axis=1, stride=1, stride_axis=0
+                ).astype(BF16)
+                gmat[lay, b, part, 0:TILE, :] = base[:, 2 * TILE:4 * TILE]
+                gmat[lay, b, part, TILE:2 * TILE, :] = base[:, TILE:3 * TILE]
+
+    def angles(lay):
+        if lay == 0:
+            @pl.when(sec != 0)
+            def _():
+                remote(screen0, screen0, ssend, srecv.at[0], me).wait_recv()
+
+            for r in range(0, 32, PIECE):
+                sine, cosine_ = sincos(screen0[r:r + PIECE, :].astype(F32))
+                sincos_ref[0, r:r + PIECE, :] = sine
+                sincos_ref[1, r:r + PIECE, :] = cosine_
+            return
+        if lay == 2:
+            own = (sec == 2) & (place // 2 == strip)
+
+            @pl.when(jnp.logical_not(own))
+            def _():
+                remote(screen2, screen2, ssend, srecv.at[2], me).wait_recv()
+
+            for r in range(0, 64, PIECE):
+                sine, cosine_ = sincos(screen2[r:r + PIECE, :].astype(F32))
+                sincos_ref[0, r:r + PIECE, :] = sine
+                sincos_ref[1, r:r + PIECE, :] = cosine_
+            return
+        ref = screen1 if lay == 1 else screen3
+
+        @pl.when(sec != lay)
+        def _():
+            remote(ref, ref, ssend, srecv.at[lay], me).wait_recv()
+
+        @pl.when(sec == lay)
+        def _():
+            some = ref.at[pl.ds(0, strips - 1)]
+            remote(some, some, ssend, srecv.at[lay], me).wait_recv()
+
+        for s in range(strips):
+            sine, cosine_ = sincos(ref[s].astype(F32))
+            sincos_ref[0, :, TILE * s:TILE * (s + 1)] = sine
+            sincos_ref[1, :, TILE * s:TILE * (s + 1)] = cosine_
+
+    def put(b, re_at, im_at, c, re, im):
+        lanes = slice(TILE * c, TILE * (c + 1))
+        re = re.astype(BF16)
+        im = im.astype(BF16)
+        slab[b, re_at:re_at + PIECE, lanes] = re
+        slab[b, im_at:im_at + PIECE, lanes] = im
+        swapped[b, re_at:re_at + PIECE, lanes] = -im
+        swapped[b, im_at:im_at + PIECE, lanes] = re
+
+    def put_all(re_at, im_at, c, x):
+        for b, (re, im) in enumerate(spread(x)):
+            put(b, re_at, im_at, c, re, im)
+
+    def pieces(split):
+        if split:
+            return [(r, 64 + r, r) for r in range(0, 64, PIECE)]
+        return [(64 * f + r, 64 * f + 32 + r, r) for f in range(2) for r in range(0, 32, PIECE)]
+
+    def screened(x, line, c):
+        out = []
+        for q, (re, im) in enumerate(x):
+            lanes = slice(QUARTER * q + TILE * c, QUARTER * q + TILE * (c + 1))
+            sine = sincos_ref[0, line:line + PIECE, lanes]
+            cosine_ = sincos_ref[1, line:line + PIECE, lanes]
+            out.append((re * cosine_ - im * sine, re * sine + im * cosine_))
+        return out
+
+    def finished(re_at, im_at, c):
+        lanes = slice(TILE * c, TILE * (c + 1))
+        return collect([
+            (ybuf[b, re_at:re_at + PIECE, lanes], ybuf[b, im_at:im_at + PIECE, lanes])
+            for b in range(4)
+        ])
+
+    def along(lay):
+        for b in range(4):
+            ybuf[b] = jnp.dot(
+                slab[b], gmat[lay, b, 0], preferred_element_type=F32
+            ) + jnp.dot(swapped[b], gmat[lay, b, 1], preferred_element_type=F32)
+
+    lane = lax.broadcasted_iota(jnp.int32, (32, TILE), 1)
+    lower = lane < 64
+
+    def across(lay, store, targets, send, recv, slot, step):
+        dims = (((1,), (1,)), ((), ()))
+        for chunk in range(2):
+            at = slice(TILE * chunk, TILE * (chunk + 1))
+            y = [
+                lax.dot_general(
+                    gmat[lay, (4 - b) % 4, 0, at, :], slab[b], dims, preferred_element_type=F32
+                ) + lax.dot_general(
+                    gmat[lay, (4 - b) % 4, 1, at, :], swapped[b], dims, preferred_element_type=F32
+                )
+                for b in range(4)
+            ]
+            for r in range(0, TILE, 32):
+                y0, y1, y2, y3 = [v[r:r + 32, :] for v in y]
+                even, odd, both, gap = y0 + y2, y0 - y2, y1 + y3, y1 - y3
+                if step == 0:
+                    turned = jnp.where(
+                        lane % 64 < 32, -pltpu.roll(gap, TILE - 32, axis=1), pltpu.roll(gap, 32, axis=1)
+                    )
+                else:
+                    moved = pltpu.roll(gap, 64, axis=1)
+                    turned = jnp.where(lower, -moved, moved)
+                for q, v in enumerate([even + both, odd - turned, even - both, odd + turned]):
+                    store(q, chunk, r, v)
+
+            def one(i, _, chunk=chunk):
+                dev, index = targets(lax.rem(i + me, 16 if step in (0, 3) else 8), chunk)
+
+                @pl.when(dev != me)
+                def _():
+                    remote(
+                        send.at[index], recv.at[slot], xsend.at[step], xrecv.at[step], dev
+                    ).start()
+                return 0
+
+            lax.fori_loop(0, 16 if step in (0, 3) else 8, one, 0)
+
+    held = {}
+
+    def store_first(q, chunk, r, v):
+        p = 4 * q + 2 * chunk + r // 64
+        if r % 64 == 0:
+            held[q] = v
+            return
+        top, bottom = held[q], v
+        send1[p] = jnp.where(lower, top, pltpu.roll(bottom, 64, axis=1)).astype(BF16)
+        send1[group + p] = jnp.where(lower, pltpu.roll(top, 64, axis=1), bottom).astype(BF16)
+
+    def targets_first(i, chunk):
+        dev = group * (i // 8) + 4 * lax.rem(i // 2, 4) + 2 * chunk + lax.rem(i, 2)
+        return dev, dev
+
+    def store_middle(send):
+        def store(q, chunk, r, v):
+            send[4 * q + 2 * chunk + r // 64, r % 64:r % 64 + 32, :] = v.astype(BF16)
+        return store
+
+    def targets_middle(i, chunk):
+        p = 4 * (i // 2) + 2 * chunk + lax.rem(i, 2)
+        return group * half + p, p
+
+    def store_last(q, chunk, r, v):
+        send4[8 * q + 4 * chunk + r // 32] = v.astype(BF16)
+
+    def targets_last(i, chunk):
+        dev = 8 * (i // 4) + 4 * chunk + lax.rem(i, 4)
+        return dev, dev
+
+    def wait_arrival(recv, number, step):
+        some = recv.at[pl.ds(0, number)]
+        remote(some, some, xsend.at[step], xrecv.at[step], me).wait_recv()
+
+    def arrive_first():
+        recv1[me] = send1[me]
+        wait_arrival(recv1, count - 1, 0)
+        small = lax.broadcasted_iota(jnp.int32, (PIECE, TILE), 1) // 32
+        for c in range(2):
+            for r in range(0, 32, PIECE):
+                tiles = []
+                for q in range(4):
+                    g = 2 * q + c
+                    got = [recv1[4 * g + s, r:r + PIECE, :].astype(F32) for s in range(4)]
+                    outs = []
+                    for fc in range(4):
+                        out = None
+                        for s in range(4):
+                            shift = ((s - fc) * 32) % TILE
+                            moved = pltpu.roll(got[s], shift, axis=1) if shift else got[s]
+                            out = moved if out is None else jnp.where(small == s, moved, out)
+                        outs.append(out)
+                    tiles.append(outs)
+                for e in range(2):
+                    at = 32 * e + r
+                    put_all(at, 64 + at, c, [(t[2 * e], t[2 * e + 1]) for t in tiles])
+
+    low16 = lax.broadcasted_iota(jnp.int32, (PIECE, TILE), 1) < 64
+
+    def joined(recv, base, g, r):
+        one = recv[base + 2 * g, r:r + PIECE, :].astype(F32)
+        two = recv[base + 2 * g + 1, r:r + PIECE, :].astype(F32)
+        return (
+            jnp.where(low16, one, pltpu.roll(two, 64, axis=1)),
+            jnp.where(low16, pltpu.roll(one, 64, axis=1), two),
+        )
+
+    def arrive_middle(send, recv, step):
+        recv[place] = send[place]
+        wait_arrival(recv, group - 1, step)
+        for c in range(2):
+            for r in range(0, 64, PIECE):
+                put_all(r, 64 + r, c, [joined(recv, 0, 2 * q + c, r) for q in range(4)])
+
+    def arrive_last():
+        recv4[me] = send4[me]
+        wait_arrival(recv4, count - 1, 3)
+        for c in range(2):
+            for f in range(2):
+                for r in range(0, 32, PIECE):
+                    put_all(
+                        64 * f + r, 64 * f + 32 + r, c,
+                        [joined(recv4, group * f, 2 * q + c, r) for q in range(4)],
+                    )
+
+    def rescreen():
+        for c in range(2):
+            for re_at, im_at, line in pieces(True):
+                put_all(re_at, im_at, c, screened(finished(re_at, im_at, c), line, c))
+
+    build(0)
+    copies[1].wait()
+    angles(0)
+    for c in range(2):
+        for n, (re_at, im_at, line) in enumerate(pieces(False)):
+            f = n // 2
+            x = []
+            for q in range(4):
+                lanes = slice(QUARTER * q + TILE * c, QUARTER * q + TILE * (c + 1))
+                x.append((
+                    field[2 * f, line:line + PIECE, lanes].astype(F32),
+                    field[2 * f + 1, line:line + PIECE, lanes].astype(F32),
+                ))
+            put_all(re_at, im_at, c, screened(x, line, c))
+    across(0, store_first, targets_first, send1, recv1, me, 0)
+
+    for lay in range(1, layers):
+        build(lay)
+    pick = jnp.concatenate([infos[a, 0:8, :] for a in range(layers)], axis=0)
+    block_row = jnp.floor(pick * (1.0 / 64.0))
+    left = (pick - 64.0 * block_row) * 16.0
+    low_row = block_row - (2 * sec).astype(F32)
+    left = jnp.where((low_row == 0.0) | (low_row == 1.0), left, -4096.0)
+    lane_f = lane.astype(F32)
+    for k in range(SUB):
+        for t in range(8):
+            select[32 * k:32 * (k + 1), TILE * t:TILE * (t + 1)] = jnp.where(
+                lane_f + float(TILE * t - k) == left, 1.0, 0.0
+            ).astype(BF16)
+
+    angles(1)
+    arrive_first()
+    along(0)
+    rescreen()
+    across(1, store_middle(send2), targets_middle, send2, recv2, place, 1)
+    angles(2)
+    arrive_middle(send2, recv2, 1)
+    along(1)
+    rescreen()
+    across(2, store_middle(send3), targets_middle, send3, recv3, place, 2)
+    angles(3)
+    arrive_middle(send3, recv3, 2)
+    along(2)
+    rescreen()
+    across(3, store_last, targets_last, send4, recv4, me, 3)
+    arrive_last()
+    along(3)
+    own = pl.ds(pl.multiple_of(32 * sec, 32), 32)
+    for c in range(2):
+        for n, (re_at, im_at, line) in enumerate(pieces(False)):
+            f = n // 2
+            for q, (re, im) in enumerate(finished(re_at, im_at, c)):
+                lanes = slice(QUARTER * q + TILE * c, QUARTER * q + TILE * (c + 1))
+                mine[re_at:re_at + PIECE, lanes] = re.astype(BF16)
+                mine[im_at:im_at + PIECE, lanes] = im.astype(BF16)
+    for fc in range(4):
+        out_ref[fc, own, :] = mine[32 * fc:32 * (fc + 1), :]
+    for k in range(1, layers):
+        peer = strip * layers + lax.rem(sec + k, layers)
+        for fc in range(4):
+            remote(
+                out_ref.at[fc, own], out_ref.at[fc, own], osend, orecv, peer
+            ).start()
+
+    copies[3].wait()
+    lane_row = lax.rem(lane // SUB, 2)
+    match = lane_row.astype(F32) == low_row
+    dims = (((1,), (1,)), ((), ()))
+    taken = lax.dot_general(select[...], mine[...], dims, preferred_element_type=F32)
+    folds = []
+    for k in range(0, SUB, 2):
+        x = jnp.where(match, taken[32 * k:32 * (k + 1), :], 0.0)
+        x2 = jnp.where(match, taken[32 * (k + 1):32 * (k + 2), :], 0.0)
+        x = x + pltpu.roll(x, TILE - SUB, axis=1)
+        x2 = x2 + pltpu.roll(x2, SUB, axis=1)
+        folds.append(jnp.where(lane_row == 0, x, x2))
+    for m in range(4):
+        c0, c1 = folds[2 * m], folds[2 * m + 1]
+        lanes = slice(TILE * m, TILE * (m + 1))
+        flat[0:32, lanes] = jnp.where(lower, c0, pltpu.roll(c1, 64, axis=1)).astype(BF16)
+        flat[32:64, lanes] = jnp.where(lower, pltpu.roll(c0, 64, axis=1), c1).astype(BF16)
+    total = jnp.zeros((64, 16), F32)
+    for n in range(4):
+        at = slice(256 * n, 256 * (n + 1))
+        past = slice(1024 + 256 * n, 1024 + 256 * (n + 1))
+        re = jnp.dot(flat[...], spot[:, at], preferred_element_type=F32)
+        im = jnp.dot(flat[...], spot[:, past], preferred_element_type=F32)
+        total = total + jnp.dot(
+            (re * re + im * im).astype(BF16), templates_ref[at, :], preferred_element_type=F32
+        )
+    for f in range(2):
+        results[:, f, 0:16] = total[32 * f:32 * (f + 1), :]
+
+    def answer(i, _):
+        dev = lax.rem(me + i, count)
+        index = 8 * lax.rem(dev, layers) + dev // layers
+        remote(results.at[index], answers.at[me], csend, crecv, dev).start()
+        return 0
+
+    lax.fori_loop(1, count, answer, 0)
+    answers[me] = results[8 * sec + strip]
+
+    most = out_ref.at[:, pl.ds(0, 96)]
+    remote(most, most, osend, orecv, me).wait()
+    some = answers.at[pl.ds(0, count - 1)]
+    remote(some, some, csend, crecv, me).wait()
+    for s in range(strips):
+        block = answers[layers * s]
+        for a in range(1, layers):
+            block = block + answers[layers * s + a]
+        corr_ref[s] = block[0:2, 0:16]
+
+    some = infos.at[pl.ds(0, layers - 1)]
+    remote(some, some, isend, irecv, me).wait_send()
+
+    @pl.when(sec == 0)
+    def _():
+        some = stage.at[pl.ds(0, 96)]
+        remote(some, some, ssend, srecv.at[0], me).wait_send()
+
+    @pl.when(lax.rem(sec, 2) == 1)
+    def _():
+        some = columns.at[pl.ds(0, count - 1)]
+        remote(some, some, ssend, srecv.at[1], me).wait_send()
+
+    @pl.when(sec == 2)
+    def _():
+        own = place // 2 == strip
+
+        @pl.when(own)
+        def _():
+            some = columns.at[pl.ds(0, 24)]
+            remote(some, some, ssend, srecv.at[2], me).wait_send()
+
+        @pl.when(jnp.logical_not(own))
+        def _():
+            remote(columns, columns, ssend, srecv.at[2], me).wait_send()
+
+    for step, (send, number) in enumerate(
+        [(send1, count), (send2, group), (send3, group), (send4, count)]
+    ):
+        some = send.at[pl.ds(0, number - 1)]
+        remote(some, some, xsend.at[step], xrecv.at[step], me).wait_send()
+
+
+def fused(launch, screens, info, templates):
+    rows, length = launch.shape[2:]
+    vmem = pl.BlockSpec(memory_space=pltpu.VMEM)
+    anywhere = pl.BlockSpec(memory_space=pl.ANY)
+    dma = pltpu.SemaphoreType.DMA
+
+    def blocks(number, height):
+        return pltpu.VMEM((number, height, TILE), BF16)
+
+    return pl.pallas_call(
+        fused_kernel,
+        out_shape=(
+            jax.ShapeDtypeStruct((4, rows, length), BF16),
+            jax.ShapeDtypeStruct((8, 2, 16), F32),
+        ),
+        in_specs=[vmem, vmem, anywhere, anywhere, anywhere, anywhere],
+        out_specs=(vmem, vmem),
+        scratch_shapes=[
+            pltpu.VMEM((4, 32, length), BF16),
+            pltpu.VMEM((rows, length), F32),
+            pltpu.VMEM((length // 2, length), BF16),
+            pltpu.VMEM((512, 2048), BF16),
+            pltpu.VMEM((4, 16, TILE), F32),
+            pltpu.VMEM((8, length), F32),
+            pltpu.VMEM((4, 4, 2, QUARTER, QUARTER), BF16),
+            pltpu.VMEM((rows, length), BF16),
+            pltpu.VMEM((length, rows), BF16),
+            pltpu.VMEM((32, length), BF16),
+            pltpu.VMEM((32, 64, TILE), BF16),
+            pltpu.VMEM((64, length), BF16),
+            pltpu.VMEM((2, 64, length), F32),
+            pltpu.VMEM((4, TILE, QUARTER), BF16),
+            pltpu.VMEM((4, TILE, QUARTER), BF16),
+            pltpu.VMEM((4, TILE, QUARTER), F32),
+            blocks(32, 32), blocks(32, 32),
+            blocks(16, 64), blocks(16, 64),
+            blocks(16, 64), blocks(16, 64),
+            blocks(32, 32), blocks(32, 32),
+            pltpu.VMEM((TILE, length), BF16),
+            pltpu.VMEM((512, length), BF16),
+            pltpu.VMEM((64, 512), BF16),
+            pltpu.VMEM((32, 8, TILE), F32),
+            pltpu.VMEM((32, 8, TILE), F32),
+            dma((4,)), dma, dma, dma, dma((4,)), dma((4,)), dma((4,)), dma, dma, dma, dma,
+        ],
+        compiler_params=pltpu.CompilerParams(
+            collective_id=2, has_side_effects=True, vmem_limit_bytes=48 << 20
+        ),
+        name="fused",
+    )(
+        info, templates, launch.reshape(4, 4, 32, length), screens[0],
+        jnp.asarray(cosine_half_table(length)), jnp.asarray(spot_rows(SUB)),
+    )
+
+
+def per_device_fused(launch, screens, distance, templates, send_table, send_counts):
+    sec = lax.axis_index("layer")
+    rows, length = launch.shape[2:]
+    pick = jnp.where(sec < send_counts[0], send_table[0, :, 0], -4096).astype(F32)
+    info = jnp.concatenate([
+        jnp.broadcast_to(pick[:, None], (8, TILE)), jnp.broadcast_to(distance[:, None], (8, TILE))
+    ])
+    pupil, found = fused(launch, screens, info, templates)
+    return pupil.reshape(2, 2, rows, length), found[None, :, None]
+
+
 def per_device(launch, screens, distance, templates, send_table, send_counts):
     layers = lax.axis_size("layer")
     strips = lax.axis_size("strip")
@@ -434,8 +1032,9 @@
         P("strip", None, "layer"),
         P("strip", None),
     )
+    small = mesh.shape["layer"] == 4 and mesh.shape["strip"] == 8
     return jax.shard_map(
-        per_device,
+        per_device_fused if small else per_device,
         mesh=mesh,
         in_specs=placed,
         out_specs=(P(None, None, "strip", None), P("strip", None, "layer", None, None)),

time: 93.4 us -> 73.1 us (0.78)
  Pallas kernels: 80.9 us -> 63.1 us
  matrix products: 1.99 us -> 0 us
    pallas_call x3 -> x1, Pallas kernels: 80.9 us -> 63.1 us  [fused(): pl.pallas_call(fused_kernel, out_shape=(jax.ShapeDtypeStruct((4, rows, le...]
    unnamed x7 -> x11, local copies, waits for them, and re-layouts: 1.38 us -> 7.57 us
    transpose x2 -> x0, local copies, waits for them, and re-layouts: 4.47 us -> none  [the longest x1 2.44 us: per_device(): pupil = done.transpose(1, 0, 2, 3).reshape(fields, 2, rows, length)]
    dot_general x3 -> x0, matrix products: 1.99 us -> none  [the longest x1 1.48 us: kernel_line(): jnp.dot(jnp.concatenate([high, low]), table, preferred_element_type=F32)]
    reshape x1 -> x0, local copies, waits for them, and re-layouts: 1.09 us -> none  [per_device(): flat = blocks.reshape(strips * fields, 2 * SUB * SUB)]
where the time goes in v1:
time: 73.1 us; the launch traced here: 72.8 us
  Pallas kernels  63.1 us (86%)
  local copies, waits for them, and re-layouts  7.65 us (10%)
  between operations  1.31 us (2%)
    pallas_call x1, Pallas kernels, fused(): pl.pallas_call(fused_kernel, out_shape=(jax.ShapeDtypeStruct((4, rows, le...  63.1 us
    unnamed x11, local copies, waits for them, and re-layouts  7.57 us

profile of v1, /device:TPU:0, one launch (start us, length us, event | category | flops | bytes accessed | tf_op | source)
XLA Modules:
  0.0 72.8 jit_solution(11136590751534558356)
XLA Ops:
  1.3 0.7 fusion
  2.0 0.1 concatenate.6.info_ref
  2.0 0.9 %copy.10.templates_ref = bf16[1024,16]{1,0:T(8,128)(2,1)S(1)} copy(bf16[1024,16]{0,1:T(8,128)(2,1)} %param.11) | data formatting | bytes 65536 | tf_op args[3]
  3.0 0.0 copy-start
  3.0 1.6 %copy-done = bf16[512,2048]{1,0:T(8,128)(2,1)S(1)} copy-done((bf16[512,2048]{1,0:T(8,128)(2,1)S(1)}, bf16[512,2048]{1,0:T(8,128)(2,1)}, u32[]{:S(2)}) %copy-start) | copy-done | bytes 2097176
  4.6 0.0 copy-start.1
  4.6 1.2 %copy-done.1 = bf16[2,2,128,1024]{3,2,1,0:T(8,128)(2,1)S(1)} copy-done((bf16[2,2,128,1024]{3,2,1,0:T(8,128)(2,1)S(1)}, bf16[2,2,128,1024]{3,2,1,0:T(8,128)(2,1)}, u32[]{:S(2)}) %copy-start.1) | copy-done | bytes 1048600
  5.8 0.0 copy-start.2
  5.8 1.2 %copy-done.2 = bf16[512,1024]{1,0:T(8,128)(2,1)S(1)} copy-done((bf16[512,1024]{1,0:T(8,128)(2,1)S(1)}, bf16[512,1024]{1,0:T(8,128)(2,1)}, u32[]{:S(2)}) %copy-start.2) | copy-done | bytes 1048600
  7.0 0.0 copy-start.3
  7.0 1.0 %copy-done.3 = f32[1,128,1024]{2,1,0:T(8,128)S(1)} copy-done((f32[1,128,1024]{2,1,0:T(8,128)S(1)}, f32[1,128,1024]{2,1,0:T(8,128)}, u32[]{:S(2)}) %copy-start.3) | copy-done | bytes 524312
  8.1 63.1 %fused.1 = (bf16[4,128,1024]{2,1,0:T(8,128)(2,1)S(1)}, f32[8,2,16]{2,1,0:T(2,128)S(1)}) custom-call(f32[16,128]{1,0:T(8,128)S(1)} %concatenate.6.info_ref, bf16[1024,16]{1,0:T(8,128)(2,1)S(1)} %copy.10.templates_ref, bf16[4,4,32,1024]{3,2,1,0:T(8,128)(2,1)S(1)} %bitcast.14, f32[128,1024]{1,0:T(8,128)S(1)} %bitcast.16, bf16[512,1024]{1,0:T(8,128)(2,1)S(1)} %copy-done.2, ...), custom_call_target="tpu_custom_call" | custom-call | tf_op jit(solution)/shard_map/fused/pallas_call | solution.py:945
  71.2 1.0 %copy.15 = bf16[2,2,128,1024]{3,2,1,0:T(8,128)(2,1)} copy(bf16[2,2,128,1024]{3,2,1,0:T(8,128)(2,1)S(1)} %bitcast.15) | data formatting | bytes 2097152
  72.2 0.6 copy.16
  (1 shorter events, 0.0 us)
Async XLA Ops:
  3.0 1.6 %copy-start = (bf16[512,2048]{1,0:T(8,128)(2,1)S(1)}, bf16[512,2048]{1,0:T(8,128)(2,1)}, u32[]{:S(2)}) copy-start(bf16[512,2048]{1,0:T(8,128)(2,1)} %constant.12.clone.spot_ref) | copy-start | bytes 6291460
  4.6 1.2 %copy-start.1 = (bf16[2,2,128,1024]{3,2,1,0:T(8,128)(2,1)S(1)}, bf16[2,2,128,1024]{3,2,1,0:T(8,128)(2,1)}, u32[]{:S(2)}) copy-start(bf16[2,2,128,1024]{3,2,1,0:T(8,128)(2,1)} %param.8) | copy-start | bytes 3145732
  5.8 1.2 %copy-start.2 = (bf16[512,1024]{1,0:T(8,128)(2,1)S(1)}, bf16[512,1024]{1,0:T(8,128)(2,1)}, u32[]{:S(2)}) copy-start(bf16[512,1024]{1,0:T(8,128)(2,1)} %constant.11.clone.cosine_ref) | copy-start | bytes 3145732
  7.0 1.0 %copy-start.3 = (f32[1,128,1024]{2,1,0:T(8,128)S(1)}, f32[1,128,1024]{2,1,0:T(8,128)}, u32[]{:S(2)}) copy-start(f32[1,128,1024]{2,1,0:T(8,128)} %param.9) | copy-start | bytes 1572868

commit v2 on v1

--- a/solution.py
+++ b/solution.py
@@ -427,11 +427,11 @@
 
 
 def fused_kernel(
-    info_ref, templates_ref, launch_ref, screen_ref, cosine_ref, spot_ref, out_ref, corr_ref,
-    field, screen, cosine, spot, infos, lines_ref, gmat, stage, staget, screen0, columns, screen2,
+    table_ref, counts_ref, distance_ref, templates_far, launch_ref, screen_ref, cosine_ref, spot_ref, out_ref, corr_ref,
+    templates_ref, field, screen, cosine, spot, infos, lines_ref, gmat, stage, staget, screen0, columns, screen2,
     sincos_ref, slab, swapped, ybuf, send1, recv1, send2, recv2, send3, recv3, send4, recv4,
     mine, select, flat, results, answers,
-    lsem, isend, irecv, ssend, srecv, xsend, xrecv, osend, orecv, csend, crecv,
+    lsem, ready, isend, irecv, ssend, srecv, fsend, frecv, xsend, xrecv, osend, orecv, csend, crecv,
 ):
     layers, strips, count = 4, 8, 32
     group = count // 2
@@ -448,20 +448,20 @@
         pltpu.make_async_copy(launch_ref.at[:, sec], field, lsem.at[1]),
         pltpu.make_async_copy(cosine_ref, cosine, lsem.at[2]),
         pltpu.make_async_copy(spot_ref, spot, lsem.at[3]),
+        pltpu.make_async_copy(templates_far, templates_ref, lsem.at[4]),
     ]
     for copy in copies:
         copy.start()
 
     barrier = pltpu.get_barrier_semaphore()
-
-    def greet(k, _):
-        peer = lax.rem(me + k, count)
+    for k in range(1, layers):
         pl.semaphore_signal(
-            barrier, inc=1, device_id=(lax.rem(peer, layers), peer // layers), device_id_type=MESH
+            barrier, inc=1, device_id=(lax.rem(sec + k, layers), strip), device_id_type=MESH
         )
-        return 0
-
-    lax.fori_loop(1, count, greet, 0)
+    for k in range(1, strips):
+        pl.semaphore_signal(
+            barrier, inc=1, device_id=(sec, lax.rem(strip + k, strips)), device_id_type=MESH
+        )
 
     def remote(src, dst, ssem, rsem, dev):
         return pltpu.make_async_remote_copy(
@@ -470,7 +470,14 @@
         )
 
     results[...] = jnp.zeros_like(results)
-    infos[sec] = info_ref[...]
+    row8 = lax.broadcasted_iota(jnp.int32, (8, TILE), 0)
+    table = jnp.zeros((8, TILE), jnp.int32)
+    live = jnp.zeros((8, TILE), jnp.int32)
+    for o in range(8):
+        table = jnp.where(row8 == o, jnp.full((8, TILE), table_ref[o], jnp.int32), table)
+        live = jnp.where(row8 == o, jnp.full((8, TILE), counts_ref[o], jnp.int32), live)
+    infos[sec, 0:8, :] = jnp.where(live > sec, table, -4096).astype(F32)
+    infos[sec, 8:16, :] = jnp.full((8, TILE), distance_ref[0], F32)
     copies[0].wait()
 
     @pl.when(lax.rem(sec, 2) == 0)
@@ -481,11 +488,11 @@
     def _():
         staget[...] = screen[...].T.astype(BF16)
 
-    pl.semaphore_wait(barrier, count - 1)
+    pl.semaphore_wait(barrier, layers + strips - 2)
 
     for k in range(1, layers):
         peer = strip * layers + lax.rem(sec + k, layers)
-        remote(info_ref, infos.at[sec], isend, irecv, peer).start()
+        remote(infos.at[sec], infos.at[sec], isend, irecv, peer).start()
 
     @pl.when(sec == 0)
     def _():
@@ -495,45 +502,83 @@
             ).start()
         screen0[...] = stage[0:32, :]
 
+    for k in range(1, layers):
+        pl.semaphore_signal(
+            ready, inc=1, device_id=(lax.rem(sec + k, layers), strip), device_id_type=MESH
+        )
+
     def share_columns(dst, sem):
         def one(k, _):
-            peer = lax.rem(me + k, count)
+            other = lax.rem(place + k, group)
             remote(
-                staget.at[pl.ds(pl.multiple_of(64 * lax.rem(peer, group), 64), 64)],
-                dst.at[strip], ssend, sem, peer,
+                staget.at[pl.ds(pl.multiple_of(64 * other, 64), 64)],
+                dst.at[strip], ssend, sem, group * half + other,
             ).start()
             return 0
 
-        lax.fori_loop(1, count, one, 0)
+        lax.fori_loop(1, group, one, 0)
         dst[strip] = staget[pl.ds(pl.multiple_of(64 * place, 64), 64), :]
 
-    @pl.when(sec == 1)
-    def _():
-        share_columns(screen1, srecv.at[1])
-
-    @pl.when(sec == 2)
-    def _():
-        for k in range(4):
-            peer = group * (k // 2) + 2 * strip + k % 2
-            src = stage.at[pl.ds(64 * (k % 2), 64)]
-
-            @pl.when(peer != me)
-            def _(peer=peer, src=src):
-                remote(src, screen2, ssend, srecv.at[2], peer).start()
-
-            @pl.when(peer == me)
-            def _(src=src):
-                screen2[...] = src[...]
-
-    @pl.when(sec == 3)
-    def _():
-        share_columns(screen3, srecv.at[3])
+    twin = group * (1 - half) + place
+    near = place // 8 == half
+    mine2 = (sec == 2) & (place // 2 == strip)
+
+    def share(lay):
+        @pl.when(sec == lay)
+        def _():
+            if lay != 2:
+                share_columns(screen1 if lay == 1 else screen3, srecv.at[lay])
+                return
+            for k in range(2):
+                peer = group * half + lax.rem(2 * strip, group) + k
+                src = stage.at[pl.ds(64 * k, 64)]
+
+                @pl.when(peer != me)
+                def _(peer=peer, src=src):
+                    remote(src, screen2, ssend, srecv.at[2], peer).start()
+
+                @pl.when(peer == me)
+                def _(src=src):
+                    screen2[...] = src[...]
+
+    def pass_on(lay):
+        if lay == 2:
+            @pl.when(near & jnp.logical_not(mine2))
+            def _():
+                remote(screen2, screen2, ssend, srecv.at[2], me).wait_recv()
+
+            @pl.when(near)
+            def _():
+                remote(screen2, screen2, fsend.at[2], frecv.at[2], twin).start()
+            return
+        ref = screen1 if lay == 1 else screen3
+
+        @pl.when(sec != lay)
+        def _():
+            some = ref.at[pl.ds(0, 4)]
+            remote(some, some, ssend, srecv.at[lay], me).wait_recv()
+
+        @pl.when(sec == lay)
+        def _():
+            some = ref.at[pl.ds(0, 3)]
+            remote(some, some, ssend, srecv.at[lay], me).wait_recv()
+
+        part = ref.at[pl.ds(4 * half, 4)]
+        remote(part, part, fsend.at[lay], frecv.at[lay], twin).start()
+
+    def passed(lay):
+        if lay == 2:
+            @pl.when(jnp.logical_not(near))
+            def _():
+                remote(screen2, screen2, fsend.at[2], frecv.at[2], me).wait_recv()
+            return
+        some = (screen1 if lay == 1 else screen3).at[pl.ds(0, 4)]
+        remote(some, some, fsend.at[lay], frecv.at[lay], me).wait_recv()
 
     most = infos.at[pl.ds(0, layers - 1)]
     remote(most, most, isend, irecv, me).wait_recv()
     copies[2].wait()
 
-    row8 = lax.broadcasted_iota(jnp.int32, (8, TILE), 0)
     dist = infos[3, 8:16, :]
     for lay in range(3):
         dist = jnp.where(row8 // 2 == lay, infos[lay, 8:16, :], dist)
@@ -589,29 +634,14 @@
                 sincos_ref[0, r:r + PIECE, :] = sine
                 sincos_ref[1, r:r + PIECE, :] = cosine_
             return
+        passed(lay)
         if lay == 2:
-            own = (sec == 2) & (place // 2 == strip)
-
-            @pl.when(jnp.logical_not(own))
-            def _():
-                remote(screen2, screen2, ssend, srecv.at[2], me).wait_recv()
-
             for r in range(0, 64, PIECE):
                 sine, cosine_ = sincos(screen2[r:r + PIECE, :].astype(F32))
                 sincos_ref[0, r:r + PIECE, :] = sine
                 sincos_ref[1, r:r + PIECE, :] = cosine_
             return
         ref = screen1 if lay == 1 else screen3
-
-        @pl.when(sec != lay)
-        def _():
-            remote(ref, ref, ssend, srecv.at[lay], me).wait_recv()
-
-        @pl.when(sec == lay)
-        def _():
-            some = ref.at[pl.ds(0, strips - 1)]
-            remote(some, some, ssend, srecv.at[lay], me).wait_recv()
-
         for s in range(strips):
             sine, cosine_ = sincos(ref[s].astype(F32))
             sincos_ref[0, :, TILE * s:TILE * (s + 1)] = sine
@@ -651,11 +681,12 @@
             for b in range(4)
         ])
 
-    def along(lay):
+    def along(lay, first=0, number=TILE):
+        at = slice(first, first + number)
         for b in range(4):
-            ybuf[b] = jnp.dot(
-                slab[b], gmat[lay, b, 0], preferred_element_type=F32
-            ) + jnp.dot(swapped[b], gmat[lay, b, 1], preferred_element_type=F32)
+            ybuf[b, at, :] = jnp.dot(
+                slab[b, at, :], gmat[lay, b, 0], preferred_element_type=F32
+            ) + jnp.dot(swapped[b, at, :], gmat[lay, b, 1], preferred_element_type=F32)
 
     lane = lax.broadcasted_iota(jnp.int32, (32, TILE), 1)
     lower = lane < 64
@@ -690,12 +721,23 @@
 
                 @pl.when(dev != me)
                 def _():
+                    src, dst = (send.at[0], recv.at[0]) if step == 3 else (send, recv)
                     remote(
-                        send.at[index], recv.at[slot], xsend.at[step], xrecv.at[step], dev
+                        src.at[index], dst.at[slot], xsend.at[step], xrecv.at[step], dev
                     ).start()
                 return 0
 
             lax.fori_loop(0, 16 if step in (0, 3) else 8, one, 0)
+
+        if step == 3:
+            def late(i, _):
+                dev = lax.rem(i + me, count)
+                remote(
+                    send.at[1, dev], recv.at[1, me], xsend.at[4], xrecv.at[4], dev
+                ).start()
+                return 0
+
+            lax.fori_loop(1, count, late, 0)
 
     held = {}
 
@@ -722,7 +764,8 @@
         return group * half + p, p
 
     def store_last(q, chunk, r, v):
-        send4[8 * q + 4 * chunk + r // 32] = v.astype(BF16)
+        for n in range(2):
+            send4[n, 8 * q + 4 * chunk + r // 32] = v[16 * n:16 * (n + 1), :].astype(BF16)
 
     def targets_last(i, chunk):
         dev = 8 * (i // 4) + 4 * chunk + lax.rem(i, 4)
@@ -772,16 +815,16 @@
             for r in range(0, 64, PIECE):
                 put_all(r, 64 + r, c, [joined(recv, 0, 2 * q + c, r) for q in range(4)])
 
-    def arrive_last():
-        recv4[me] = send4[me]
-        wait_arrival(recv4, count - 1, 3)
+    def arrive_last(n):
+        recv, send = recv4.at[n], send4.at[n]
+        recv[me] = send[me]
+        wait_arrival(recv, count - 1, 3 + n)
         for c in range(2):
             for f in range(2):
-                for r in range(0, 32, PIECE):
-                    put_all(
-                        64 * f + r, 64 * f + 32 + r, c,
-                        [joined(recv4, group * f, 2 * q + c, r) for q in range(4)],
-                    )
+                at = 64 * n + 32 * f
+                put_all(
+                    at, at + 16, c, [joined(recv, group * f, 2 * q + c, 0) for q in range(4)]
+                )
 
     def rescreen():
         for c in range(2):
@@ -789,6 +832,8 @@
                 put_all(re_at, im_at, c, screened(finished(re_at, im_at, c), line, c))
 
     build(0)
+    pl.semaphore_wait(ready, layers - 1)
+    share(1)
     copies[1].wait()
     angles(0)
     for c in range(2):
@@ -804,6 +849,9 @@
             put_all(re_at, im_at, c, screened(x, line, c))
     across(0, store_first, targets_first, send1, recv1, me, 0)
 
+    share(2)
+    share(3)
+    pass_on(1)
     for lay in range(1, layers):
         build(lay)
     pick = jnp.concatenate([infos[a, 0:8, :] for a in range(layers)], axis=0)
@@ -823,6 +871,8 @@
     along(0)
     rescreen()
     across(1, store_middle(send2), targets_middle, send2, recv2, place, 1)
+    pass_on(2)
+    pass_on(3)
     angles(2)
     arrive_middle(send2, recv2, 1)
     along(1)
@@ -833,26 +883,46 @@
     along(2)
     rescreen()
     across(3, store_last, targets_last, send4, recv4, me, 3)
-    arrive_last()
-    along(3)
-    own = pl.ds(pl.multiple_of(32 * sec, 32), 32)
-    for c in range(2):
-        for n, (re_at, im_at, line) in enumerate(pieces(False)):
-            f = n // 2
-            for q, (re, im) in enumerate(finished(re_at, im_at, c)):
-                lanes = slice(QUARTER * q + TILE * c, QUARTER * q + TILE * (c + 1))
-                mine[re_at:re_at + PIECE, lanes] = re.astype(BF16)
-                mine[im_at:im_at + PIECE, lanes] = im.astype(BF16)
-    for fc in range(4):
-        out_ref[fc, own, :] = mine[32 * fc:32 * (fc + 1), :]
-    for k in range(1, layers):
-        peer = strip * layers + lax.rem(sec + k, layers)
+    beside = strip * layers + sec + 1 - 2 * lax.rem(sec, 2)
+    above = strip * layers + lax.rem(sec + 2, layers)
+
+    def rows_of(n, owner):
+        return pl.ds(pl.multiple_of(32 * owner + 16 * n, 16), 16)
+
+    def publish(n):
+        own = rows_of(n, sec)
         for fc in range(4):
-            remote(
-                out_ref.at[fc, own], out_ref.at[fc, own], osend, orecv, peer
-            ).start()
+            f, part = fc // 2, fc % 2
+            out_ref[fc, own, :] = mine[64 * f + 32 * part + 16 * n:64 * f + 32 * part + 16 * n + 16, :]
+        part = out_ref.at[:, own]
+        remote(part, part, osend.at[4 * n], orecv.at[4 * n], beside).start()
+        remote(part, part, osend.at[4 * n + 1], orecv.at[4 * n + 1], above).start()
+
+    def relay(n):
+        part = out_ref.at[:, rows_of(n, sec)]
+        remote(part, part, osend.at[4 * n], orecv.at[4 * n], me).wait_recv()
+        given = out_ref.at[pl.ds(0, 2), rows_of(n, sec + 1 - 2 * lax.rem(sec, 2))]
+        remote(given, given, osend.at[4 * n + 2], orecv.at[4 * n + 2], above).start()
+        remote(part, part, osend.at[4 * n + 1], orecv.at[4 * n + 1], me).wait_recv()
+        given = out_ref.at[pl.ds(2, 2), rows_of(n, lax.rem(sec + 2, layers))]
+        remote(given, given, osend.at[4 * n + 3], orecv.at[4 * n + 3], beside).start()
+
+    for n in range(2):
+        arrive_last(n)
+        along(3, 64 * n, 64)
+        for c in range(2):
+            for f in range(2):
+                at = 64 * n + 32 * f
+                for q, (re, im) in enumerate(finished(at, at + 16, c)):
+                    lanes = slice(QUARTER * q + TILE * c, QUARTER * q + TILE * (c + 1))
+                    to = 64 * f + 16 * n
+                    mine[to:to + PIECE, lanes] = re.astype(BF16)
+                    mine[to + 32:to + 32 + PIECE, lanes] = im.astype(BF16)
+        publish(n)
+    relay(0)
 
     copies[3].wait()
+    copies[4].wait()
     lane_row = lax.rem(lane // SUB, 2)
     match = lane_row.astype(F32) == low_row
     dims = (((1,), (1,)), ((), ()))
@@ -875,8 +945,8 @@
         past = slice(1024 + 256 * n, 1024 + 256 * (n + 1))
         re = jnp.dot(flat[...], spot[:, at], preferred_element_type=F32)
         im = jnp.dot(flat[...], spot[:, past], preferred_element_type=F32)
-        total = total + jnp.dot(
-            (re * re + im * im).astype(BF16), templates_ref[at, :], preferred_element_type=F32
+        total = total + lax.dot_general(
+            (re * re + im * im).astype(BF16), templates_ref[:, at], dims, preferred_element_type=F32
         )
     for f in range(2):
         results[:, f, 0:16] = total[32 * f:32 * (f + 1), :]
@@ -890,8 +960,13 @@
     lax.fori_loop(1, count, answer, 0)
     answers[me] = results[8 * sec + strip]
 
-    most = out_ref.at[:, pl.ds(0, 96)]
-    remote(most, most, osend, orecv, me).wait()
+    relay(1)
+    for n in range(2):
+        part = out_ref.at[:, rows_of(n, sec)]
+        for k in range(2):
+            remote(part, part, osend.at[4 * n + k], orecv.at[4 * n + k], me).wait_send()
+            given = out_ref.at[pl.ds(0, 2), rows_of(n, sec)]
+            remote(given, given, osend.at[4 * n + 2 + k], orecv.at[4 * n + 2 + k], me).wait()
     some = answers.at[pl.ds(0, count - 1)]
     remote(some, some, csend, crecv, me).wait()
     for s in range(strips):
@@ -910,33 +985,37 @@
 
     @pl.when(lax.rem(sec, 2) == 1)
     def _():
-        some = columns.at[pl.ds(0, count - 1)]
+        some = columns.at[pl.ds(0, group - 1)]
         remote(some, some, ssend, srecv.at[1], me).wait_send()
 
-    @pl.when(sec == 2)
+    @pl.when((sec == 2) & mine2)
     def _():
-        own = place // 2 == strip
-
-        @pl.when(own)
-        def _():
-            some = columns.at[pl.ds(0, 24)]
-            remote(some, some, ssend, srecv.at[2], me).wait_send()
-
-        @pl.when(jnp.logical_not(own))
-        def _():
-            remote(columns, columns, ssend, srecv.at[2], me).wait_send()
+        remote(screen2, screen2, ssend, srecv.at[2], me).wait_send()
+
+    @pl.when((sec == 2) & jnp.logical_not(mine2))
+    def _():
+        remote(stage, stage, ssend, srecv.at[2], me).wait_send()
+
+    @pl.when(near)
+    def _():
+        remote(screen2, screen2, fsend.at[2], frecv.at[2], me).wait_send()
+
+    for lay, ref in ((1, screen1), (3, screen3)):
+        some = ref.at[pl.ds(0, 4)]
+        remote(some, some, fsend.at[lay], frecv.at[lay], me).wait_send()
 
     for step, (send, number) in enumerate(
-        [(send1, count), (send2, group), (send3, group), (send4, count)]
+        [(send1, count), (send2, group), (send3, group), (send4.at[0], count), (send4.at[1], count)]
     ):
         some = send.at[pl.ds(0, number - 1)]
         remote(some, some, xsend.at[step], xrecv.at[step], me).wait_send()
 
 
-def fused(launch, screens, info, templates):
+def fused(launch, screens, distance, templates, send_table, send_counts):
     rows, length = launch.shape[2:]
     vmem = pl.BlockSpec(memory_space=pltpu.VMEM)
-    anywhere = pl.BlockSpec(memory_space=pl.ANY)
+    smem = pl.BlockSpec(memory_space=pltpu.SMEM)
+    far = pl.BlockSpec(memory_space=pltpu.HBM)
     dma = pltpu.SemaphoreType.DMA
 
     def blocks(number, height):
@@ -948,9 +1027,10 @@
             jax.ShapeDtypeStruct((4, rows, length), BF16),
             jax.ShapeDtypeStruct((8, 2, 16), F32),
         ),
-        in_specs=[vmem, vmem, anywhere, anywhere, anywhere, anywhere],
+        in_specs=[smem, smem, smem, far, far, far, far, far],
         out_specs=(vmem, vmem),
         scratch_shapes=[
+            pltpu.VMEM(templates.shape[::-1], BF16),
             pltpu.VMEM((4, 32, length), BF16),
             pltpu.VMEM((rows, length), F32),
             pltpu.VMEM((length // 2, length), BF16),
@@ -961,7 +1041,7 @@
             pltpu.VMEM((rows, length), BF16),
             pltpu.VMEM((length, rows), BF16),
             pltpu.VMEM((32, length), BF16),
-            pltpu.VMEM((32, 64, TILE), BF16),
+            pltpu.VMEM((16, 64, TILE), BF16),
             pltpu.VMEM((64, length), BF16),
             pltpu.VMEM((2, 64, length), F32),
             pltpu.VMEM((4, TILE, QUARTER), BF16),
@@ -970,32 +1050,28 @@
             blocks(32, 32), blocks(32, 32),
             blocks(16, 64), blocks(16, 64),
             blocks(16, 64), blocks(16, 64),
-            blocks(32, 32), blocks(32, 32),
+            pltpu.VMEM((2, 32, 16, TILE), BF16), pltpu.VMEM((2, 32, 16, TILE), BF16),
             pltpu.VMEM((TILE, length), BF16),
             pltpu.VMEM((512, length), BF16),
             pltpu.VMEM((64, 512), BF16),
-            pltpu.VMEM((32, 8, TILE), F32),
-            pltpu.VMEM((32, 8, TILE), F32),
-            dma((4,)), dma, dma, dma, dma((4,)), dma((4,)), dma((4,)), dma, dma, dma, dma,
+            pltpu.VMEM((32, 2, TILE), F32),
+            pltpu.VMEM((32, 2, TILE), F32),
+            dma((5,)), pltpu.SemaphoreType.REGULAR, dma, dma, dma, dma((4,)), dma((4,)), dma((4,)),
+            dma((5,)), dma((5,)), dma((8,)), dma((8,)), dma, dma,
         ],
         compiler_params=pltpu.CompilerParams(
-            collective_id=2, has_side_effects=True, vmem_limit_bytes=48 << 20
+            collective_id=2, has_side_effects=True, vmem_limit_bytes=60 << 20
         ),
         name="fused",
     )(
-        info, templates, launch.reshape(4, 4, 32, length), screens[0],
+        send_table.reshape(8), send_counts.reshape(8), distance, templates.T, launch.reshape(4, 4, 32, length), screens[0],
         jnp.asarray(cosine_half_table(length)), jnp.asarray(spot_rows(SUB)),
     )
 
 
 def per_device_fused(launch, screens, distance, templates, send_table, send_counts):
-    sec = lax.axis_index("layer")
     rows, length = launch.shape[2:]
-    pick = jnp.where(sec < send_counts[0], send_table[0, :, 0], -4096).astype(F32)
-    info = jnp.concatenate([
-        jnp.broadcast_to(pick[:, None], (8, TILE)), jnp.broadcast_to(distance[:, None], (8, TILE))
-    ])
-    pupil, found = fused(launch, screens, info, templates)
+    pupil, found = fused(launch, screens, distance, templates, send_table, send_counts)
     return pupil.reshape(2, 2, rows, length), found[None, :, None]
 
 

time: 73.1 us -> 61.2 us (0.84)
  Pallas kernels: 63.1 us -> 56.9 us
  local copies, waits for them, and re-layouts: 7.65 us -> 2.87 us
    pallas_call x1, Pallas kernels: 63.1 us -> 56.9 us  [fused(): pl.pallas_call(fused_kernel, out_shape=(jax.ShapeDtypeStruct((4, rows, le...]
    unnamed x11 -> x4, local copies, waits for them, and re-layouts: 7.57 us -> 2.87 us
where the time goes in v2:
time: 61.2 us; the launch traced here: 61 us
  Pallas kernels  56.9 us (93%)
  local copies, waits for them, and re-layouts  2.87 us (5%)
  between operations  1.29 us (2%)
    pallas_call x1, Pallas kernels, fused(): pl.pallas_call(fused_kernel, out_shape=(jax.ShapeDtypeStruct((4, rows, le...  56.9 us
    unnamed x4, local copies, waits for them, and re-layouts  2.87 us

profile of v2, /device:TPU:0, one launch (start us, length us, event | category | flops | bytes accessed | tf_op | source)
XLA Modules:
  0.0 61.0 jit_solution(5793366409612607948)
XLA Ops:
  1.3 56.9 %fused.1 = (bf16[4,128,1024]{2,1,0:T(8,128)(2,1)}, f32[8,2,16]{2,1,0:T(2,128)}) custom-call(s32[8]{0:T(128)} %bitcast.14, s32[8]{0:T(128)} %bitcast.15, f32[1]{0:T(128)S(6)} %copy.13.distance_ref, bf16[16,1024]{1,0:T(8,128)(2,1)} %bitcast.12, bf16[4,4,32,1024]{3,2,1,0:T(8,128)(2,1)} %bitcast.10, f32[128,1024]{1,0:T(8,128)} %bitcast.11, ...), custom_call_target="tpu_custom_call" | custom-call | tf_op jit(solution)/shard_map/fused/pallas_call | solution.py:1024
  58.2 0.0 copy-start
  58.2 2.3 %copy.14 = bf16[2,2,128,1024]{3,2,1,0:T(8,128)(2,1)} copy(bf16[2,2,128,1024]{3,2,1,0:T(8,128)(2,1)} %bitcast.9) | data formatting | bytes 2097152
  60.4 0.0 copy-done
  60.4 0.6 copy.15
Async XLA Ops:
  58.2 2.3 %copy-start = (f32[8,2,16]{2,1,0:T(2,128)S(1)}, f32[8,2,16]{2,1,0:T(2,128)}, u32[]{:S(2)}) copy-start(f32[8,2,16]{2,1,0:T(2,128)} %get-tuple-element.5) | copy-start | bytes 3076

commit v3 on v2

--- a/solution.py
+++ b/solution.py
@@ -428,7 +428,7 @@
 
 def fused_kernel(
     table_ref, counts_ref, distance_ref, templates_far, launch_ref, screen_ref, cosine_ref, spot_ref, out_ref, corr_ref,
-    templates_ref, field, screen, cosine, spot, infos, lines_ref, gmat, stage, staget, screen0, columns, screen2,
+    templates_ref, field, screen, cosine, spot, infos, lines_ref, gmat, stage, staget, hops, screen0, columns, screen2,
     sincos_ref, slab, swapped, ybuf, send1, recv1, send2, recv2, send3, recv3, send4, recv4,
     mine, select, flat, results, answers,
     lsem, ready, isend, irecv, ssend, srecv, fsend, frecv, xsend, xrecv, osend, orecv, csend, crecv,
@@ -486,9 +486,74 @@
 
     @pl.when(lax.rem(sec, 2) == 1)
     def _():
-        staget[...] = screen[...].T.astype(BF16)
+        staget[...] = screen[...].T.astype(BF16).reshape(4, 4, 64, TILE)
 
     pl.semaphore_wait(barrier, layers + strips - 2)
+
+    twin = group * (1 - half) + place
+    near = place // 8 == half
+    mine2 = (sec == 2) & (place // 2 == strip)
+
+    def share(lay):
+        @pl.when(sec == lay)
+        def _():
+            if lay != 2:
+                for k in range(1, layers):
+                    a = (lay + k) % layers
+                    remote(
+                        staget.at[:, a], hops.at[lay // 2], ssend, srecv.at[lay], strip * layers + a
+                    ).start()
+                hops[lay // 2] = staget[:, lay]
+                return
+            for k in range(2):
+                peer = group * half + lax.rem(2 * strip, group) + k
+                src = stage.at[pl.ds(64 * k, 64)]
+
+                @pl.when(peer != me)
+                def _(peer=peer, src=src):
+                    remote(src, screen2, ssend, srecv.at[2], peer).start()
+
+                @pl.when(peer == me)
+                def _(src=src):
+                    screen2[...] = src[...]
+
+    def pass_on(lay):
+        if lay == 2:
+            @pl.when(near & jnp.logical_not(mine2))
+            def _():
+                remote(screen2, screen2, ssend, srecv.at[2], me).wait_recv()
+
+            @pl.when(near)
+            def _():
+                remote(screen2, screen2, fsend.at[2], frecv.at[2], twin).start()
+            return
+        ref = screen1 if lay == 1 else screen3
+
+        hop = hops.at[lay // 2]
+
+        @pl.when(sec != lay)
+        def _():
+            remote(hop, hop, ssend, srecv.at[lay], me).wait_recv()
+
+        def one(k, _):
+            other = lax.rem(strip + k, strips)
+            remote(
+                hop.at[lax.rem(other, 4)], ref.at[strip], fsend.at[lay], frecv.at[lay],
+                other * layers + sec,
+            ).start()
+            return 0
+
+        lax.fori_loop(1, strips, one, 0)
+        ref[strip] = hop[lax.rem(strip, 4)]
+
+    def passed(lay):
+        if lay == 2:
+            @pl.when(jnp.logical_not(near))
+            def _():
+                remote(screen2, screen2, fsend.at[2], frecv.at[2], me).wait_recv()
+            return
+        some = (screen1 if lay == 1 else screen3).at[pl.ds(0, strips - 1)]
+        remote(some, some, fsend.at[lay], frecv.at[lay], me).wait_recv()
 
     for k in range(1, layers):
         peer = strip * layers + lax.rem(sec + k, layers)
@@ -502,78 +567,12 @@
             ).start()
         screen0[...] = stage[0:32, :]
 
+    share(1)
+
     for k in range(1, layers):
         pl.semaphore_signal(
             ready, inc=1, device_id=(lax.rem(sec + k, layers), strip), device_id_type=MESH
         )
-
-    def share_columns(dst, sem):
-        def one(k, _):
-            other = lax.rem(place + k, group)
-            remote(
-                staget.at[pl.ds(pl.multiple_of(64 * other, 64), 64)],
-                dst.at[strip], ssend, sem, group * half + other,
-            ).start()
-            return 0
-
-        lax.fori_loop(1, group, one, 0)
-        dst[strip] = staget[pl.ds(pl.multiple_of(64 * place, 64), 64), :]
-
-    twin = group * (1 - half) + place
-    near = place // 8 == half
-    mine2 = (sec == 2) & (place // 2 == strip)
-
-    def share(lay):
-        @pl.when(sec == lay)
-        def _():
-            if lay != 2:
-                share_columns(screen1 if lay == 1 else screen3, srecv.at[lay])
-                return
-            for k in range(2):
-                peer = group * half + lax.rem(2 * strip, group) + k
-                src = stage.at[pl.ds(64 * k, 64)]
-
-                @pl.when(peer != me)
-                def _(peer=peer, src=src):
-                    remote(src, screen2, ssend, srecv.at[2], peer).start()
-
-                @pl.when(peer == me)
-                def _(src=src):
-                    screen2[...] = src[...]
-
-    def pass_on(lay):
-        if lay == 2:
-            @pl.when(near & jnp.logical_not(mine2))
-            def _():
-                remote(screen2, screen2, ssend, srecv.at[2], me).wait_recv()
-
-            @pl.when(near)
-            def _():
-                remote(screen2, screen2, fsend.at[2], frecv.at[2], twin).start()
-            return
-        ref = screen1 if lay == 1 else screen3
-
-        @pl.when(sec != lay)
-        def _():
-            some = ref.at[pl.ds(0, 4)]
-            remote(some, some, ssend, srecv.at[lay], me).wait_recv()
-
-        @pl.when(sec == lay)
-        def _():
-            some = ref.at[pl.ds(0, 3)]
-            remote(some, some, ssend, srecv.at[lay], me).wait_recv()
-
-        part = ref.at[pl.ds(4 * half, 4)]
-        remote(part, part, fsend.at[lay], frecv.at[lay], twin).start()
-
-    def passed(lay):
-        if lay == 2:
-            @pl.when(jnp.logical_not(near))
-            def _():
-                remote(screen2, screen2, fsend.at[2], frecv.at[2], me).wait_recv()
-            return
-        some = (screen1 if lay == 1 else screen3).at[pl.ds(0, 4)]
-        remote(some, some, fsend.at[lay], frecv.at[lay], me).wait_recv()
 
     most = infos.at[pl.ds(0, layers - 1)]
     remote(most, most, isend, irecv, me).wait_recv()
@@ -832,9 +831,8 @@
                 put_all(re_at, im_at, c, screened(finished(re_at, im_at, c), line, c))
 
     build(0)
-    pl.semaphore_wait(ready, layers - 1)
-    share(1)
     copies[1].wait()
+    pass_on(1)
     angles(0)
     for c in range(2):
         for n, (re_at, im_at, line) in enumerate(pieces(False)):
@@ -847,11 +845,11 @@
                     field[2 * f + 1, line:line + PIECE, lanes].astype(F32),
                 ))
             put_all(re_at, im_at, c, screened(x, line, c))
+    pl.semaphore_wait(ready, layers - 1)
     across(0, store_first, targets_first, send1, recv1, me, 0)
 
     share(2)
     share(3)
-    pass_on(1)
     for lay in range(1, layers):
         build(lay)
     pick = jnp.concatenate([infos[a, 0:8, :] for a in range(layers)], axis=0)
@@ -894,18 +892,20 @@
         for fc in range(4):
             f, part = fc // 2, fc % 2
             out_ref[fc, own, :] = mine[64 * f + 32 * part + 16 * n:64 * f + 32 * part + 16 * n + 16, :]
-        part = out_ref.at[:, own]
-        remote(part, part, osend.at[4 * n], orecv.at[4 * n], beside).start()
-        remote(part, part, osend.at[4 * n + 1], orecv.at[4 * n + 1], above).start()
+        for k in range(2):
+            part = out_ref.at[pl.ds(2 * k, 2), own]
+            remote(part, part, osend.at[n, 0, k], orecv.at[n, 0, k], beside).start()
+            part = out_ref.at[pl.ds(2 - 2 * k, 2), own]
+            remote(part, part, osend.at[n, 1, k], orecv.at[n, 1, k], above).start()
 
     def relay(n):
-        part = out_ref.at[:, rows_of(n, sec)]
-        remote(part, part, osend.at[4 * n], orecv.at[4 * n], me).wait_recv()
+        part = out_ref.at[pl.ds(0, 2), rows_of(n, sec)]
+        remote(part, part, osend.at[n, 0, 0], orecv.at[n, 0, 0], me).wait_recv()
         given = out_ref.at[pl.ds(0, 2), rows_of(n, sec + 1 - 2 * lax.rem(sec, 2))]
-        remote(given, given, osend.at[4 * n + 2], orecv.at[4 * n + 2], above).start()
-        remote(part, part, osend.at[4 * n + 1], orecv.at[4 * n + 1], me).wait_recv()
+        remote(given, given, osend.at[n, 2, 0], orecv.at[n, 2, 0], above).start()
+        remote(part, part, osend.at[n, 1, 0], orecv.at[n, 1, 0], me).wait_recv()
         given = out_ref.at[pl.ds(2, 2), rows_of(n, lax.rem(sec + 2, layers))]
-        remote(given, given, osend.at[4 * n + 3], orecv.at[4 * n + 3], beside).start()
+        remote(given, given, osend.at[n, 2, 1], orecv.at[n, 2, 1], beside).start()
 
     for n in range(2):
         arrive_last(n)
@@ -962,11 +962,13 @@
 
     relay(1)
     for n in range(2):
-        part = out_ref.at[:, rows_of(n, sec)]
+        part = out_ref.at[pl.ds(0, 2), rows_of(n, sec)]
         for k in range(2):
-            remote(part, part, osend.at[4 * n + k], orecv.at[4 * n + k], me).wait_send()
-            given = out_ref.at[pl.ds(0, 2), rows_of(n, sec)]
-            remote(given, given, osend.at[4 * n + 2 + k], orecv.at[4 * n + 2 + k], me).wait()
+            for way in range(3):
+                copy = remote(part, part, osend.at[n, way, k], orecv.at[n, way, k], me)
+                copy.wait_send()
+                if way == 2 or k == 1:
+                    copy.wait_recv()
     some = answers.at[pl.ds(0, count - 1)]
     remote(some, some, csend, crecv, me).wait()
     for s in range(strips):
@@ -985,7 +987,7 @@
 
     @pl.when(lax.rem(sec, 2) == 1)
     def _():
-        some = columns.at[pl.ds(0, group - 1)]
+        some = columns.at[pl.ds(0, 12)]
         remote(some, some, ssend, srecv.at[1], me).wait_send()
 
     @pl.when((sec == 2) & mine2)
@@ -1001,7 +1003,7 @@
         remote(screen2, screen2, fsend.at[2], frecv.at[2], me).wait_send()
 
     for lay, ref in ((1, screen1), (3, screen3)):
-        some = ref.at[pl.ds(0, 4)]
+        some = ref.at[pl.ds(0, strips - 1)]
         remote(some, some, fsend.at[lay], frecv.at[lay], me).wait_send()
 
     for step, (send, number) in enumerate(
@@ -1039,7 +1041,8 @@
             pltpu.VMEM((8, length), F32),
             pltpu.VMEM((4, 4, 2, QUARTER, QUARTER), BF16),
             pltpu.VMEM((rows, length), BF16),
-            pltpu.VMEM((length, rows), BF16),
+            pltpu.VMEM((4, 4, 64, TILE), BF16),
+            pltpu.VMEM((2, 4, 64, TILE), BF16),
             pltpu.VMEM((32, length), BF16),
             pltpu.VMEM((16, 64, TILE), BF16),
             pltpu.VMEM((64, length), BF16),
@@ -1057,7 +1060,7 @@
             pltpu.VMEM((32, 2, TILE), F32),
             pltpu.VMEM((32, 2, TILE), F32),
             dma((5,)), pltpu.SemaphoreType.REGULAR, dma, dma, dma, dma((4,)), dma((4,)), dma((4,)),
-            dma((5,)), dma((5,)), dma((8,)), dma((8,)), dma, dma,
+            dma((5,)), dma((5,)), dma((2, 3, 2)), dma((2, 3, 2)), dma, dma,
         ],
         compiler_params=pltpu.CompilerParams(
             collective_id=2, has_side_effects=True, vmem_limit_bytes=60 << 20
@@ -1069,9 +1072,42 @@
     )
 
 
+def finish_kernel(pupil_ref, found_ref, pupil_out, found_out, pupil, found, gets, puts):
+    pairs = [(found_ref, found, found_out)]
+    pairs += [(pupil_ref.at[n], pupil.at[n], pupil_out.at[n]) for n in range(4)]
+    reads = [pltpu.make_async_copy(s, m, gets.at[n]) for n, (s, m, _) in enumerate(pairs)]
+    writes = [pltpu.make_async_copy(m, d, puts.at[n]) for n, (_, m, d) in enumerate(pairs)]
+    for copy in reads:
+        copy.start()
+    for read, write in zip(reads, writes):
+        read.wait()
+        write.start()
+    for write in writes:
+        write.wait()
+
+
+def finish(pupil, found):
+    far = pl.BlockSpec(memory_space=pltpu.HBM)
+    dma = pltpu.SemaphoreType.DMA
+    return pl.pallas_call(
+        finish_kernel,
+        out_shape=tuple(jax.ShapeDtypeStruct(x.shape, x.dtype) for x in (pupil, found)),
+        in_specs=[far, far],
+        out_specs=(far, far),
+        scratch_shapes=[
+            pltpu.VMEM(pupil.shape, pupil.dtype), pltpu.VMEM(found.shape, found.dtype),
+            dma((5,)), dma((5,)),
+        ],
+        compiler_params=pltpu.CompilerParams(vmem_limit_bytes=60 << 20),
+        name="finish",
+    )(pupil, found)
+
+
 def per_device_fused(launch, screens, distance, templates, send_table, send_counts):
     rows, length = launch.shape[2:]
-    pupil, found = fused(launch, screens, distance, templates, send_table, send_counts)
+    pupil, found = finish(
+        *fused(launch, screens, distance, templates, send_table, send_counts)
+    )
     return pupil.reshape(2, 2, rows, length), found[None, :, None]
 
 

time: 61.2 us -> 58.9 us (0.962)
  local copies, waits for them, and re-layouts: 2.87 us -> 0 us
    unnamed x4 -> x0, local copies, waits for them, and re-layouts: 2.87 us -> none
    pallas_call x0 -> x1, Pallas kernels: none -> 2.01 us  [finish(): pl.pallas_call(finish_kernel, out_shape=tuple((jax.ShapeDtypeStruct(x.sha...]
    pallas_call x1, Pallas kernels: 56.9 us -> 55.3 us  [fused(): pl.pallas_call(fused_kernel, out_shape=(jax.ShapeDtypeStruct((4, rows, le...]
where the time goes in v3:
time: 58.9 us; the launch traced here: 58.6 us
  Pallas kernels  57.3 us (97%)
  between operations  1.28 us (2%)
    pallas_call x1, Pallas kernels, fused(): pl.pallas_call(fused_kernel, out_shape=(jax.ShapeDtypeStruct((4, rows, le...  55.3 us
    pallas_call x1, Pallas kernels, finish(): pl.pallas_call(finish_kernel, out_shape=tuple((jax.ShapeDtypeStruct(x.sha...  2.01 us

profile of v3, /device:TPU:0, one launch (start us, length us, event | category | flops | bytes accessed | tf_op | source)
XLA Modules:
  0.0 58.6 jit_solution(1734196565804507830)
XLA Ops:
  1.3 55.3 %fused.1 = (bf16[4,128,1024]{2,1,0:T(8,128)(2,1)}, f32[8,2,16]{2,1,0:T(2,128)}) custom-call(s32[8]{0:T(128)} %bitcast.12, s32[8]{0:T(128)} %bitcast.13, f32[1]{0:T(128)S(6)} %copy.11.distance_ref, bf16[16,1024]{1,0:T(8,128)(2,1)} %bitcast.11, bf16[4,4,32,1024]{3,2,1,0:T(8,128)(2,1)} %bitcast.9, f32[128,1024]{1,0:T(8,128)} %bitcast.10, ...), custom_call_target="tpu_custom_call" | custom-call | tf_op jit(solution)/shard_map/fused/pallas_call | solution.py:1026
  56.6 2.0 %finish.1 = (bf16[4,128,1024]{2,1,0:T(8,128)(2,1)}, f32[8,2,16]{2,1,0:T(2,128)}) custom-call(bf16[4,128,1024]{2,1,0:T(8,128)(2,1)} %get-tuple-element.6.pupil_ref, f32[8,2,16]{2,1,0:T(2,128)} %get-tuple-element.7.found_ref), custom_call_target="tpu_custom_call" | custom-call | tf_op jit(solution)/shard_map/finish/pallas_call | solution.py:1092

commit v4 on v3

--- a/solution.py
+++ b/solution.py
@@ -430,8 +430,8 @@
     table_ref, counts_ref, distance_ref, templates_far, launch_ref, screen_ref, cosine_ref, spot_ref, out_ref, corr_ref,
     templates_ref, field, screen, cosine, spot, infos, lines_ref, gmat, stage, staget, hops, screen0, columns, screen2,
     sincos_ref, slab, swapped, ybuf, send1, recv1, send2, recv2, send3, recv3, send4, recv4,
-    mine, select, flat, results, answers,
-    lsem, ready, isend, irecv, ssend, srecv, fsend, frecv, xsend, xrecv, osend, orecv, csend, crecv,
+    mine, pupil, select, flat, results, answers,
+    lsem, ready, isend, irecv, ssend, srecv, fsend, frecv, xsend, xrecv, osend, orecv, csend, crecv, wsem,
 ):
     layers, strips, count = 4, 8, 32
     group = count // 2
@@ -887,25 +887,34 @@
     def rows_of(n, owner):
         return pl.ds(pl.multiple_of(32 * owner + 16 * n, 16), 16)
 
+    def keep(first, number, rows):
+        part = (pl.ds(first, number), rows)
+        pltpu.make_async_copy(pupil.at[part], out_ref.at[part], wsem).start()
+
     def publish(n):
         own = rows_of(n, sec)
         for fc in range(4):
             f, part = fc // 2, fc % 2
-            out_ref[fc, own, :] = mine[64 * f + 32 * part + 16 * n:64 * f + 32 * part + 16 * n + 16, :]
+            pupil[fc, own, :] = mine[64 * f + 32 * part + 16 * n:64 * f + 32 * part + 16 * n + 16, :]
         for k in range(2):
-            part = out_ref.at[pl.ds(2 * k, 2), own]
+            part = pupil.at[pl.ds(2 * k, 2), own]
             remote(part, part, osend.at[n, 0, k], orecv.at[n, 0, k], beside).start()
-            part = out_ref.at[pl.ds(2 - 2 * k, 2), own]
+            part = pupil.at[pl.ds(2 - 2 * k, 2), own]
             remote(part, part, osend.at[n, 1, k], orecv.at[n, 1, k], above).start()
+        keep(0, 4, own)
 
     def relay(n):
-        part = out_ref.at[pl.ds(0, 2), rows_of(n, sec)]
+        part = pupil.at[pl.ds(0, 2), rows_of(n, sec)]
         remote(part, part, osend.at[n, 0, 0], orecv.at[n, 0, 0], me).wait_recv()
-        given = out_ref.at[pl.ds(0, 2), rows_of(n, sec + 1 - 2 * lax.rem(sec, 2))]
+        rows = rows_of(n, sec + 1 - 2 * lax.rem(sec, 2))
+        given = pupil.at[pl.ds(0, 2), rows]
         remote(given, given, osend.at[n, 2, 0], orecv.at[n, 2, 0], above).start()
+        keep(0, 2, rows)
         remote(part, part, osend.at[n, 1, 0], orecv.at[n, 1, 0], me).wait_recv()
-        given = out_ref.at[pl.ds(2, 2), rows_of(n, lax.rem(sec + 2, layers))]
+        rows = rows_of(n, lax.rem(sec + 2, layers))
+        given = pupil.at[pl.ds(2, 2), rows]
         remote(given, given, osend.at[n, 2, 1], orecv.at[n, 2, 1], beside).start()
+        keep(2, 2, rows)
 
     for n in range(2):
         arrive_last(n)
@@ -962,13 +971,11 @@
 
     relay(1)
     for n in range(2):
-        part = out_ref.at[pl.ds(0, 2), rows_of(n, sec)]
-        for k in range(2):
-            for way in range(3):
-                copy = remote(part, part, osend.at[n, way, k], orecv.at[n, way, k], me)
-                copy.wait_send()
-                if way == 2 or k == 1:
-                    copy.wait_recv()
+        part = pupil.at[pl.ds(0, 2), rows_of(n, sec)]
+        owners = (sec + 1 - 2 * lax.rem(sec, 2), lax.rem(sec + 2, layers), layers - 1 - sec)
+        for way, k, first in ((0, 1, 2), (1, 1, 0), (2, 0, 0), (2, 1, 2)):
+            remote(part, part, osend.at[n, way, k], orecv.at[n, way, k], me).wait_recv()
+            keep(first, 2, rows_of(n, owners[way]))
     some = answers.at[pl.ds(0, count - 1)]
     remote(some, some, csend, crecv, me).wait()
     for s in range(strips):
@@ -977,6 +984,13 @@
             block = block + answers[layers * s + a]
         corr_ref[s] = block[0:2, 0:16]
 
+    part = pupil.at[pl.ds(0, 2), rows_of(0, sec)]
+    for n in range(2):
+        for k in range(2):
+            for way in range(3):
+                remote(part, part, osend.at[n, way, k], orecv.at[n, way, k], me).wait_send()
+    pltpu.make_async_copy(pupil, out_ref, wsem).wait()
+
     some = infos.at[pl.ds(0, layers - 1)]
     remote(some, some, isend, irecv, me).wait_send()
 
@@ -1030,7 +1044,7 @@
             jax.ShapeDtypeStruct((8, 2, 16), F32),
         ),
         in_specs=[smem, smem, smem, far, far, far, far, far],
-        out_specs=(vmem, vmem),
+        out_specs=(far, vmem),
         scratch_shapes=[
             pltpu.VMEM(templates.shape[::-1], BF16),
             pltpu.VMEM((4, 32, length), BF16),
@@ -1055,12 +1069,13 @@
             blocks(16, 64), blocks(16, 64),
             pltpu.VMEM((2, 32, 16, TILE), BF16), pltpu.VMEM((2, 32, 16, TILE), BF16),
             pltpu.VMEM((TILE, length), BF16),
+            pltpu.VMEM((4, rows, length), BF16),
             pltpu.VMEM((512, length), BF16),
             pltpu.VMEM((64, 512), BF16),
             pltpu.VMEM((32, 2, TILE), F32),
             pltpu.VMEM((32, 2, TILE), F32),
             dma((5,)), pltpu.SemaphoreType.REGULAR, dma, dma, dma, dma((4,)), dma((4,)), dma((4,)),
-            dma((5,)), dma((5,)), dma((2, 3, 2)), dma((2, 3, 2)), dma, dma,
+            dma((5,)), dma((5,)), dma((2, 3, 2)), dma((2, 3, 2)), dma, dma, dma,
         ],
         compiler_params=pltpu.CompilerParams(
             collective_id=2, has_side_effects=True, vmem_limit_bytes=60 << 20

time: 58.9 us -> 59.1 us (level)
  no operation moved by 1% of the time
where the time goes in v4:
time: 59.1 us; the launch traced here: 58.8 us
  Pallas kernels  57.5 us (97%)
  between operations  1.28 us (2%)
    pallas_call x1, Pallas kernels, fused(): pl.pallas_call(fused_kernel, out_shape=(jax.ShapeDtypeStruct((4, rows, le...  55.5 us
    pallas_call x1, Pallas kernels, finish(): pl.pallas_call(finish_kernel, out_shape=tuple((jax.ShapeDtypeStruct(x.sha...  2.01 us

profile of v4, /device:TPU:0, one launch (start us, length us, event | category | flops | bytes accessed | tf_op | source)
XLA Modules:
  0.0 58.8 jit_solution(8644311501682087041)
XLA Ops:
  1.3 55.5 %fused.1 = (bf16[4,128,1024]{2,1,0:T(8,128)(2,1)}, f32[8,2,16]{2,1,0:T(2,128)}) custom-call(s32[8]{0:T(128)} %bitcast.12, s32[8]{0:T(128)} %bitcast.13, f32[1]{0:T(128)S(6)} %copy.11.distance_ref, bf16[16,1024]{1,0:T(8,128)(2,1)} %bitcast.11, bf16[4,4,32,1024]{3,2,1,0:T(8,128)(2,1)} %bitcast.9, f32[128,1024]{1,0:T(8,128)} %bitcast.10, ...), custom_call_target="tpu_custom_call" | custom-call | tf_op jit(solution)/shard_map/fused/pallas_call | solution.py:1040
  56.8 2.0 %finish.1 = (bf16[4,128,1024]{2,1,0:T(8,128)(2,1)}, f32[8,2,16]{2,1,0:T(2,128)}) custom-call(bf16[4,128,1024]{2,1,0:T(8,128)(2,1)} %get-tuple-element.6.pupil_ref, f32[8,2,16]{2,1,0:T(2,128)} %get-tuple-element.7.found_ref), custom_call_target="tpu_custom_call" | custom-call | tf_op jit(solution)/shard_map/finish/pallas_call | solution.py:1107
